TPU v7x, 32 devices: a whole 2x2x4 slice. The times are simulated.
32 devices in a mesh: gen: 4 (over x, core), bank: 8 (over z, y).
Axes of the slice: x: 2, y: 2, z: 4, core: 2. Of those that a mesh axis runs over, the one named last changes fastest.
Arguments:
- latents: bfloat16 [2048, 4096], P(('gen', 'bank')), may hold values from -6 to 6
- shift: bfloat16 [2048, 4096], P(('gen', 'bank')), may hold values from -3 to 3
- scale_mod: bfloat16 [2048, 4096], P(('gen', 'bank')), may hold values from -3 to 3
- head_weight: bfloat16 [4096, 1024], P('gen'), may hold values from -0.09375 to 0.09375
- bank: bfloat16 [16384, 1024], P('bank'), may hold values from -8 to 8
Outputs:
- update: float32 [4096, 1024], P(('gen', 'bank'))
All inputs are finite; a program needn't handle non-finite values.
Results may differ from a plain program's by a relative error of at most 0.0042.
Values may be sent and summed in bfloat16 or wider, within the bound.
No kernel may reach another device: no remote copies, remote signals or barrier semaphores. Data moves between devices by JAX's collectives and lax.ppermute only.
A program may use at most 128 MiB of HBM per device.

v0:
```python
import jax
import jax.numpy as jnp
from jax import lax
from jax.experimental import pallas as pl
from jax.experimental.pallas import tpu as pltpu
from jax.sharding import PartitionSpec as P

kernel_scale = 32.0
F32, BF16 = jnp.float32, jnp.bfloat16
GEN, BANK = "gen", "bank"
VMEM = pl.BlockSpec(memory_space=pltpu.VMEM)
HBM = pl.BlockSpec(memory_space=pltpu.HBM)


def swap(value, axis, mask):
    count = lax.axis_size(axis)
    return lax.ppermute(value, axis, [(i, i ^ mask) for i in range(count)])


def here():
    gen, bank = lax.axis_index(GEN), lax.axis_index(BANK)
    return gen >> 1, gen & 1, bank >> 1, bank & 1


def call(body, arrays, outs, flops, scratch=(), to_hbm=False, from_hbm=0):
    far_away = [i >= len(arrays) - from_hbm for i in range(len(arrays))]
    arrays = [
        pltpu.with_memory_space_constraint(a, pltpu.HBM if there else pltpu.VMEM)
        for a, there in zip(arrays, far_away)
    ]
    make = jax.ShapeDtypeStruct if to_hbm else pltpu.VMEM
    size = sum(a.size * a.dtype.itemsize for a in arrays)
    return pl.pallas_call(
        body,
        in_specs=[HBM if there else VMEM for there in far_away],
        out_specs=[HBM if to_hbm else VMEM] * len(outs),
        out_shape=[make(dims, dtype) for dims, dtype in outs],
        scratch_shapes=list(scratch),
        compiler_params=pltpu.CompilerParams(vmem_limit_bytes=24 << 20),
        cost_estimate=pl.CostEstimate(flops=flops, bytes_accessed=size, transcendentals=0),
    )(*arrays)


def modulate(latents, shift, scale_mod, bank):
    samples, depth = latents.shape
    rows = 16
    quarter = depth // 4
    steps = samples // rows
    forward, direct = shares(bank.shape[0])

    def body(*refs):
        place = here()
        sources, bank_hbm = refs[:3], refs[3]
        hid_ref, lent_ref, own_ref, f_ref, d_ref = refs[4:9]
        held, sems, row_sems = refs[9:12], refs[12], refs[13]
        side, core = place[0], place[1]
        copies = [
            [
                pltpu.make_async_copy(src.at[pl.ds(r * rows, rows)], dst.at[r], sems.at[i, r])
                for i, (src, dst) in enumerate(zip(sources, held))
            ]
            for r in range(steps)
        ]
        starts = (2 * side + core) * forward, 4 * forward + core * direct
        sent = [
            pltpu.make_async_copy(
                bank_hbm.at[pl.ds(pl.multiple_of(start, 16), ref.shape[0])], ref, row_sems.at[i]
            )
            for i, (start, ref) in enumerate(zip(starts, (f_ref, d_ref)))
        ]
        for group in copies + [sent]:
            for copy in group:
                copy.start()
        for r in range(steps):
            for copy in copies[r]:
                copy.wait()
            at = slice(r * rows, (r + 1) * rows)
            x, b, s = (ref[r].astype(F32) for ref in held)
            inverse = lax.rsqrt(jnp.mean(x * x, axis=1, keepdims=True) + 1e-06)
            hid_ref[at] = (x * inverse * (1.0 + s) + b).astype(BF16)
        for ref, s in ((lent_ref, 1 - side), (own_ref, side)):
            for i, c in enumerate((core, 1 - core)):
                start = pl.multiple_of((2 * s + c) * quarter, quarter)
                ref[:, i * quarter : (i + 1) * quarter] = hid_ref[:, pl.ds(start, quarter)]
        for copy in sent:
            copy.wait()

    half = (samples, depth // 2)
    width = bank.shape[1]
    return call(
        body,
        [latents, shift, scale_mod, bank],
        [
            ((samples, depth), BF16),
            (half, BF16),
            (half, BF16),
            ((forward, width), BF16),
            ((direct, width), BF16),
        ],
        8 * samples * depth,
        [pltpu.VMEM((steps, rows, depth), BF16)] * 3
        + [pltpu.SemaphoreType.DMA((3, steps)), pltpu.SemaphoreType.DMA((2,))],
        from_hbm=4,
    )


def project(lent, own, first, second):
    samples = own.shape[0]
    quarter, width = first.shape

    def body(x_ref, y_ref, w_ref, v_ref, lent_ref, own_ref, held):
        held[:samples] = x_ref[...]
        held[samples:] = y_ref[...]
        total = jnp.dot(
            held[:, :quarter], w_ref[...], preferred_element_type=F32
        ) + jnp.dot(held[:, quarter:], v_ref[...], preferred_element_type=F32)
        lent_ref[...] = total[:samples]
        own_ref[...] = total[samples:]

    return call(
        body,
        [lent, own, first, second],
        [((samples, width), F32)] * 2,
        8 * samples * quarter * width,
        [pltpu.VMEM((2 * samples, 2 * quarter), BF16)],
    )


def finish_embed(part, other):
    def body(a_ref, b_ref, exact_ref, unit_ref, length_ref):
        embed = a_ref[...] + b_ref[...].astype(F32)
        length = jnp.sqrt(jnp.sum(embed * embed, axis=1, keepdims=True) + 1e-06)
        exact = embed / length
        exact_ref[...] = exact
        unit_ref[...] = exact.astype(BF16)
        length_ref[...] = jnp.broadcast_to(length, length_ref.shape)

    samples, width = part.shape
    return call(
        body,
        [part, other],
        [((samples, width), F32), ((samples, width), BF16), ((samples, 128), F32)],
        6 * samples * width,
    )


def shares(rows):
    return 11 * rows // 64, 10 * rows // 64


def unit_rows(x):
    x = x.astype(F32)
    return (x / jnp.sqrt(jnp.sum(x * x, axis=1, keepdims=True) + 1e-06)).astype(BF16)


def normalize_sent(forward, direct):
    size = forward.shape[0] // 2
    width = forward.shape[1]

    def body(a_ref, b_ref, e_ref, f_ref, d_ref):
        e_ref[...] = unit_rows(a_ref[:size])
        f_ref[...] = unit_rows(a_ref[size:])
        d_ref[...] = unit_rows(b_ref[...])

    return call(
        body,
        [forward, direct],
        [((size, width), BF16)] * 2 + [(direct.shape, BF16)],
        8 * (forward.size + direct.size),
    )


def stage(hidden, weight, n_bank):
    samples, depth = hidden.shape
    pair = depth // 4 // n_bank * 2
    count = n_bank // 2 if pair % 256 == 0 else 0

    def body(hid_ref, w_hbm, o_ref, *refs):
        place = here()
        copy = pltpu.make_async_copy(w_hbm, o_ref, refs[-1])
        copy.start()
        for i, ref in enumerate(refs[:-1]):
            for g in range(4):
                start = pl.multiple_of(g * (depth // 4) + (place[2] ^ i) * pair, pair)
                ref[:, g * pair : (g + 1) * pair] = hid_ref[:, pl.ds(start, pair)]
        copy.wait()

    weight, *pieces = call(
        body,
        [hidden, weight],
        [(weight.shape, BF16)] + [((samples, 4 * pair), BF16)] * count,
        0,
        [pltpu.SemaphoreType.DMA(())],
        from_hbm=1,
    )
    return weight, pieces


def normalize(bank):
    rows, width = bank.shape
    steps = 8
    tile = rows // steps

    def body(x_hbm, o_ref, x_ref, sems):
        copies = [
            pltpu.make_async_copy(x_hbm.at[pl.ds(i * tile, tile)], x_ref.at[i], sems.at[i])
            for i in range(steps)
        ]
        for copy in copies:
            copy.start()
        for i in range(steps):
            copies[i].wait()
            o_ref[i * tile : (i + 1) * tile] = unit_rows(x_ref[i])

    return call(
        body,
        [bank],
        [(bank.shape, BF16)],
        8 * bank.size,
        [pltpu.VMEM((steps, tile, width), BF16), pltpu.SemaphoreType.DMA((steps,))],
        from_hbm=1,
    )[0]


def join(pieces):
    samples, width = pieces[0].shape
    count = len(pieces)

    def body(*refs):
        for i in range(count):
            refs[-1][i * samples : (i + 1) * samples] = refs[i][...]

    return call(body, pieces, [((count * samples, width), BF16)], 0)[0]


def bank_sums(line, blocks, before=None, samples=None):
    total, width = line.shape
    count = 1 if samples is None else total // samples

    def body(*refs):
        line_ref, rest = refs[0], refs[1:]
        row_refs, rest = rest[: len(blocks)], rest[len(blocks) :]
        held = None if before is None else rest[0]
        outs = rest[-count - (count > 1) :][:count]
        sums = rest[-1]
        for block, ref in zip(blocks, row_refs):
            tile = min(1024, block.shape[0])
            for start in range(0, block.shape[0], tile):
                rows = ref[start : start + tile]
                scores = lax.dot_general(
                    line_ref[...], rows, (((1,), (1,)), ((), ())), preferred_element_type=F32
                )
                weight = jnp.exp(kernel_scale * scores).astype(BF16)
                term = jnp.dot(weight, rows, preferred_element_type=F32)
                sums[...] = term if held is None else held[...] + term
                held = sums
        if count > 1:
            for i, ref in enumerate(outs):
                ref[...] = sums[i * samples : (i + 1) * samples].astype(ref.dtype)

    dims = (total // count, width)
    return call(
        body,
        [line] + list(blocks) + ([] if before is None else [before]),
        [(dims, BF16 if i else F32) for i in range(count)],
        4 * total * width * sum(block.shape[0] for block in blocks),
        [pltpu.VMEM((total, width), F32)] * (count > 1),
    )


def pair_sums(unit, line, across):
    samples, width = unit.shape
    batch = 2 * line.shape[0]

    def body(unit_ref, line_ref, across_ref, out_ref):
        total = 0.0
        for ref, first in ((line_ref, True), (across_ref, False)):
            scores = lax.dot_general(
                unit_ref[...], ref[...], (((1,), (1,)), ((), ())), preferred_element_type=F32
            )
            weight = jnp.exp(kernel_scale * scores)
            if first:
                same = lax.broadcasted_iota(
                    jnp.int32, scores.shape, 0
                ) == lax.broadcasted_iota(jnp.int32, scores.shape, 1)
                weight = jnp.where(same, 0.0, weight)
            total = total + jnp.dot(
                weight.astype(BF16), ref[...], preferred_element_type=F32
            )
        out_ref[...] = total / (batch - 1)

    return call(
        body,
        [unit, line, across],
        [((samples, width), F32)],
        4 * samples * width * batch,
    )[0]


def embed_gradient(near, far, parts, exact, length, bank_rows):
    count = len(parts)
    samples, width = near.shape
    half = width // 2

    def body(*refs):
        place = here()
        near_ref, far_ref, exact_ref, length_ref = refs[:4]
        keep_ref, give_ref = refs[-2:]
        total = far_ref[...]
        for ref in refs[4 : 4 + count]:
            total = total + ref[...].astype(F32)
        proof = near_ref[...] - total / bank_rows
        exact = exact_ref[...]
        radial = jnp.sum(exact * proof, axis=1, keepdims=True)
        grad = (proof - exact * radial) / length_ref[:, :1]
        first = place[0] == 0
        left, right = grad[:, :half], grad[:, half:]
        keep_ref[...] = jnp.where(first, left, right).astype(BF16)
        give_ref[...] = jnp.where(first, right, left).astype(BF16)

    return call(
        body,
        [near, far, exact, length] + list(parts),
        [((samples, half), BF16)] * 2,
        (count + 8) * samples * width,
    )


def split_pairs(pieces):
    samples, width = pieces[0].shape
    block = width // 8
    count = len(pieces)

    def body(*refs):
        place = here()
        ins, outs = refs[:count], refs[count:]
        for out, y in zip(outs, (place[3], 1 - place[3])):
            for i, ref in enumerate(ins):
                for g in range(4):
                    start = pl.multiple_of((2 * g + y) * block, block)
                    out[i * samples : (i + 1) * samples, g * block : (g + 1) * block] = ref[
                        :, pl.ds(start, block)
                    ]

    return call(
        body, pieces, [((count * samples, 4 * block), BF16)] * 2, 0
    )


def turn(kept, given):
    rows, width = kept.shape

    def body(a_ref, b_ref, o_ref):
        o_ref[:, :rows] = a_ref[...].T
        o_ref[:, rows:] = b_ref[...].T

    return call(body, [kept, given], [((width, 2 * rows), BF16)], 0)[0]


def feature_sums(columns, grads, core):
    fresh = len(grads) > 1
    arrays = [array for group in grads for array in group]
    samples = sum(array.shape[0] for array in grads[0]) // 2
    width = arrays[0].shape[1]
    batch = len(grads) * samples
    piece = columns[0].shape[0] // 4

    def body(own_ref, other_ref, *refs):
        place = here()
        outs = refs[len(arrays) :]
        held = outs[-1] if fresh else refs[0]
        if fresh:
            ins = iter(refs)
            for i, group in enumerate(grads):
                own = next(ins)
                if len(group) > 1:
                    own, other = own[...], next(ins)[...]
                else:
                    own, other = own[:samples], own[samples:]
                held[i * samples : (i + 1) * samples] = own
                held[batch + i * samples : batch + (i + 1) * samples] = other
        for side in (0, 1):
            start = 2 * (place[0] ^ side) + (place[1] ^ core)
            start = pl.multiple_of(start * piece, piece)
            outs[0][side * piece : (side + 1) * piece] = jnp.dot(
                own_ref[pl.ds(start, piece), :], held[:batch], preferred_element_type=F32
            ) + jnp.dot(
                other_ref[pl.ds(start, piece), :], held[batch:], preferred_element_type=F32
            )

    return call(
        body,
        list(columns) + arrays,
        [((2 * piece, width), F32)] + [((2 * batch, width), BF16)] * fresh,
        8 * piece * width * batch,
    )


def square_sums(kept, taken, devices):
    rows, width = kept.shape[0] // 2, kept.shape[1]

    def body(a_ref, b_ref, home_ref, away_ref, out_ref):
        total = 0.0
        for ref, at in ((home_ref, slice(0, rows)), (away_ref, slice(rows, 2 * rows))):
            block = a_ref[at] + b_ref[at]
            ref[...] = block
            total = total + jnp.sum((block * block).reshape(rows // 8, 8, width), axis=0)
        tile = total[:, :128]
        for i in range(1, width // 128):
            tile = tile + total[:, i * 128 : (i + 1) * 128]
        tile = jnp.sum(tile, axis=0, keepdims=True)
        out_ref[...] = jnp.broadcast_to(tile[None], out_ref.shape)

    return call(
        body,
        [kept, taken],
        [((rows, width), F32)] * 2 + [((devices, 1, 128), F32)],
        8 * rows * width,
    )


def scaled(home, other, squares, entries):
    rows, half = home.shape
    steps = 4 if rows % 32 == 0 else 1
    size = rows // steps

    def body(h_ref, a_ref, s_ref, o_hbm, held, sems):
        place = here()
        mean = jnp.sum(s_ref[...]) / entries
        factor = lax.rsqrt(jnp.full((1, 1), mean + 1e-06, F32))
        copies = []
        for i in range(steps):
            at = slice(i * size, (i + 1) * size)
            first = place[0] == 0
            held[at, :half] = jnp.where(first, h_ref[at], a_ref[at]) * factor
            held[at, half:] = jnp.where(first, a_ref[at], h_ref[at]) * factor
            copies.append(
                pltpu.make_async_copy(held.at[at], o_hbm.at[pl.ds(i * size, size)], sems.at[i])
            )
            copies[-1].start()
        for copy in copies:
            copy.wait()

    dims = (rows, 2 * half)
    return call(
        body,
        [home, other, squares],
        [(dims, F32)],
        2 * home.size,
        [pltpu.VMEM(dims, F32), pltpu.SemaphoreType.DMA((steps,))],
        to_hbm=True,
    )[0]


def by_feature(hidden, pieces, n_bank):
    samples, depth = hidden.shape
    piece = depth // 4 // n_bank
    if pieces:
        pieces = [swap(p, BANK, 2 * i) if i else p for i, p in enumerate(pieces)]
        kept, given = split_pairs(pieces)
        given = swap(given, BANK, 1)
        return turn(kept, given)
    place = here()
    pairs = hidden.reshape(samples, 4, n_bank // 2, 2 * piece)
    pieces = [
        lax.dynamic_index_in_dim(pairs, place[2] ^ i, 2, keepdims=False)
        for i in range(n_bank // 2)
    ]
    pieces = [swap(p, BANK, 2 * i) if i else p for i, p in enumerate(pieces)]
    columns = jnp.concatenate(pieces, 0)
    kept = lax.dynamic_slice_in_dim(columns, place[3] * piece, piece, 2)
    given = swap(lax.dynamic_slice_in_dim(columns, (1 - place[3]) * piece, piece, 2), BANK, 1)
    return jnp.concatenate([kept, given], 0).reshape(n_bank * samples, 4 * piece).T


def local(latents, shift, scale_mod, head_weight, bank):
    samples, depth = latents.shape
    width = head_weight.shape[1]
    n_gen = lax.axis_size(GEN)
    n_bank = lax.axis_size(BANK)
    evens, odds = list(range(0, n_bank, 2)), list(range(1, n_bank, 2))

    head_other = swap(head_weight, GEN, 1)
    hidden, lent, own, forward, direct = modulate(latents, shift, scale_mod, bank)
    lent = swap(lent, GEN, 2)
    *forward, direct = normalize_sent(forward, direct)
    head_weight, pieces = stage(hidden, head_weight, n_bank)
    bank_unit = normalize(bank)
    lent_part, own_part = project(lent, own, head_weight, head_other)
    returned = swap(lent_part, GEN, 2)
    exact, unit, length = finish_embed(own_part, returned)

    columns = by_feature(hidden, pieces, n_bank)

    forward = [swap(v, BANK, 1) for v in forward]
    direct = swap(direct, BANK, 1)
    beside = [swap(v, GEN, 2) for v in forward]
    forward, beside = join(forward), join(beside)
    early = [forward, swap(forward, GEN, 1)]
    middle = [beside, direct]
    late = [swap(v, GEN, 1) for v in middle]

    line = [unit] + [swap(unit, BANK, m) for m in evens[1:]]
    line = join(line)
    across = swap(line, BANK, 1)
    sums = bank_sums(line, [bank_unit] + early)[0]
    sums = bank_sums(line, middle, sums)[0]
    far = bank_sums(line, late, sums, samples)
    parts = [swap(v, BANK, m) for m, v in zip(evens[1:], far[1:])]
    near = pair_sums(unit, line, across)
    keep, give = embed_gradient(
        near, far[0], parts, exact, length, bank.shape[0] * n_bank
    )

    given = swap(give, GEN, 2)
    both = join([keep, given])
    high = range(n_bank - 2, n_bank // 2 - 1, -2)
    grads = {0: [keep, given]}
    for m in high:
        grads[m] = [swap(keep, BANK, m)]
    for m in high:
        grads[m].append(swap(given, BANK, m))
    for m in range(n_bank // 2 - 1, 0, -1):
        grads[m] = [swap(both, BANK, m)]
    for m in high:
        ahead = grads[m]
        grads[m + 1] = [swap(v, BANK, 1) for v in ahead]
    grads = [grads[m] for m in evens + odds]
    columns = [columns, swap(columns, GEN, 2)]
    for_core, grads = feature_sums(columns, grads, 1)
    taken = swap(for_core, GEN, 1)
    kept = feature_sums(columns, [[grads]], 0)[0]
    home, away, squares = square_sums(kept, taken, n_gen * n_bank)
    away = swap(away, GEN, 2)
    squares = lax.all_to_all(squares, (GEN, BANK), 0, 0, tiled=True)
    return scaled(home, away, squares, depth * width)


def solution(mesh):
    placed = (
        P((GEN, BANK), None),
        P((GEN, BANK), None),
        P((GEN, BANK), None),
        P(GEN, None),
        P(BANK, None),
    )
    return jax.shard_map(
        lambda *args: local(*args),
        mesh=mesh,
        in_specs=placed,
        out_specs=P((GEN, BANK), None),
        check_vma=False,
    )
```

profile of v0, /device:TPU:0, one launch (start us, length us, event | category | flops | bytes accessed | tf_op | source)
XLA Modules:
  0.0 126.6 jit_solution(8356557376597468205)
XLA Ops:
  0.5 2.0 %shard_map.55 = (bf16[64,4096]{1,0:T(8,128)(2,1)S(1)}, bf16[64,2048]{1,0:T(8,128)(2,1)S(1)}, bf16[64,2048]{1,0:T(8,128)(2,1)S(1)}, bf16[352,1024]{1,0:T(8,128)(2,1)S(1)}, bf16[320,1024]{1,0:T(8,128)(2,1)S(1)}) custom-call(bf16[64,4096]{1,0:T(8,128)(2,1)} %refs_0_.1, bf16[64,4096]{1,0:T(8,128)(2,1)} %refs_1_.1, bf16[64,4096]{1,0:T(8,128)(2,1)} %refs_2_.1, ...), custom_call_target="tpu_custom_call" | custom-call | flops 2097152 | bytes 5767168 | tf_op jit(solution)/shard_map/pallas_call | solution.py:33
  3.0 2.6 %collective-permute-start.12 = (bf16[176,1024]{1,0:T(8,128)(2,1)S(1)}, bf16[176,1024]{1,0:T(8,128)(2,1)S(1)}, u32[]{:S(2)}, u32[]{:S(2)}) collective-permute-start(bf16[176,1024]{1,0:T(8,128)(2,1)S(1)} %get-tuple-element.51), channel_id=1, source_target_pairs={{0,1},{1,0},{2,3},{3,2},{4,5},{5,4},{6,7},{7,6},{8,9},{9,8},{10,11... | collective-permute-start | bytes 1081352 | tf_op jit(solution)/shard_map/ppermute | solution.py:17
  5.7 1.9 %collective-permute-start.5 = (bf16[64,2048]{1,0:T(8,128)(2,1)S(1)}, bf16[64,2048]{1,0:T(8,128)(2,1)S(1)}, u32[]{:S(2)}, u32[]{:S(2)}) collective-permute-start(bf16[64,2048]{1,0:T(8,128)(2,1)S(1)} %get-tuple-element.43), channel_id=1, source_target_pairs={{0,16},{8,24},{16,0},{24,8},{1,17},{9,25},{17,1},{25,9},{2,18},{10... | collective-permute-start | bytes 786440 | tf_op jit(solution)/shard_map/ppermute | solution.py:17
  7.6 1.5 %collective-permute-start.17 = (bf16[320,1024]{1,0:T(8,128)(2,1)S(1)}, bf16[320,1024]{1,0:T(8,128)(2,1)S(1)}, u32[]{:S(2)}, u32[]{:S(2)}) collective-permute-start(bf16[320,1024]{1,0:T(8,128)(2,1)S(1)} %get-tuple-element.53), channel_id=1, source_target_pairs={{0,1},{1,0},{2,3},{3,2},{4,5},{5,4},{6,7},{7,6},{8,9},{9,8},{10,11... | collective-permute-start | bytes 1966088 | tf_op jit(solution)/shard_map/ppermute | solution.py:17
  9.1 5.7 %collective-permute-done.12.refs_0_ = bf16[176,1024]{1,0:T(8,128)(2,1)S(1)} collective-permute-done((bf16[176,1024]{1,0:T(8,128)(2,1)S(1)}, bf16[176,1024]{1,0:T(8,128)(2,1)S(1)}, u32[]{:S(2)}, u32[]{:S(2)}) %collective-permute-start.12) | collective-permute-done | bytes 360480 | tf_op jit(solution)/shard_map/ppermute | solution.py:17
  14.9 2.0 %collective-permute-start.13 = (bf16[176,1024]{1,0:T(8,128)(2,1)S(1)}, bf16[176,1024]{1,0:T(8,128)(2,1)S(1)}, u32[]{:S(2)}, u32[]{:S(2)}) collective-permute-start(bf16[176,1024]{1,0:T(8,128)(2,1)S(1)} %collective-permute-done.12.refs_0_), channel_id=1, source_target_pairs={{0,16},{8,24},{16,0},{24,8},{1,17},{9,25},{17,1},{25,9},{2,18},{10... | collective-permute-start | bytes 1081352 | tf_op jit(solution)/shard_map/ppermute | solution.py:17
  16.9 1.6 %shard_map.56 = (bf16[1024,1024]{1,0:T(8,128)(2,1)S(1)}, bf16[64,1024]{1,0:T(8,128)(2,1)S(1)}, bf16[64,1024]{1,0:T(8,128)(2,1)S(1)}, bf16[64,1024]{1,0:T(8,128)(2,1)S(1)}, bf16[64,1024]{1,0:T(8,128)(2,1)S(1)}) custom-call(bf16[64,4096]{1,0:T(8,128)(2,1)S(1)} %get-tuple-element.36.hid_ref, bf16[1024,1024]{1,0:T(8,128)(2,1)} %w_hbm.1), custom_call_target="tpu_custom_call" | custom-call | bytes 2621440 | tf_op jit(solution)/shard_map/pallas_call | solution.py:33
  18.5 1.6 %collective-permute-start = (bf16[64,1024]{1,0:T(8,128)(2,1)S(1)}, bf16[64,1024]{1,0:T(8,128)(2,1)S(1)}, u32[]{:S(2)}, u32[]{:S(2)}) collective-permute-start(bf16[64,1024]{1,0:T(8,128)(2,1)S(1)} %get-tuple-element.38), channel_id=1, source_target_pairs={{0,2},{1,3},{2,0},{3,1},{4,6},{5,7},{6,4},{7,5},{8,10},{9,11},{10,... | collective-permute-start | bytes 393224 | tf_op jit(solution)/shard_map/ppermute | solution.py:17
  20.1 2.5 %collective-permute-done.14.refs_1_ = bf16[176,1024]{1,0:T(8,128)(2,1)S(1)} collective-permute-done((bf16[176,1024]{1,0:T(8,128)(2,1)S(1)}, bf16[176,1024]{1,0:T(8,128)(2,1)S(1)}, u32[]{:S(2)}, u32[]{:S(2)}) %collective-permute-start.14) | collective-permute-done | bytes 360480 | tf_op jit(solution)/shard_map/ppermute | solution.py:17
  22.6 2.0 %collective-permute-start.15 = (bf16[176,1024]{1,0:T(8,128)(2,1)S(1)}, bf16[176,1024]{1,0:T(8,128)(2,1)S(1)}, u32[]{:S(2)}, u32[]{:S(2)}) collective-permute-start(bf16[176,1024]{1,0:T(8,128)(2,1)S(1)} %collective-permute-done.14.refs_1_), channel_id=1, source_target_pairs={{0,16},{8,24},{16,0},{24,8},{1,17},{9,25},{17,1},{25,9},{2,18},{10... | collective-permute-start | bytes 1081352 | tf_op jit(solution)/shard_map/ppermute | solution.py:17
  25.6 3.1 %collective-permute-start.1 = (bf16[64,1024]{1,0:T(8,128)(2,1)S(1)}, bf16[64,1024]{1,0:T(8,128)(2,1)S(1)}, u32[]{:S(2)}, u32[]{:S(2)}) collective-permute-start(bf16[64,1024]{1,0:T(8,128)(2,1)S(1)} %get-tuple-element.39), channel_id=1, source_target_pairs={{0,4},{1,5},{2,6},{3,7},{4,0},{5,1},{6,2},{7,3},{8,12},{9,13},{10,... | collective-permute-start | bytes 393224 | tf_op jit(solution)/shard_map/ppermute | solution.py:17
  28.7 9.6 %collective-permute-done.7.b_ref = f32[64,1024]{1,0:T(8,128)S(1)} collective-permute-done((f32[64,1024]{1,0:T(8,128)S(1)}, f32[64,1024]{1,0:T(8,128)S(1)}, u32[]{:S(2)}, u32[]{:S(2)}) %collective-permute-start.7) | collective-permute-done | bytes 262176 | tf_op jit(solution)/shard_map/ppermute | solution.py:17
  38.3 3.5 %collective-permute-start.2 = (bf16[64,1024]{1,0:T(8,128)(2,1)S(1)}, bf16[64,1024]{1,0:T(8,128)(2,1)S(1)}, u32[]{:S(2)}, u32[]{:S(2)}) collective-permute-start(bf16[64,1024]{1,0:T(8,128)(2,1)S(1)} %get-tuple-element.40), channel_id=1, source_target_pairs={{0,6},{1,7},{2,4},{3,5},{4,2},{5,3},{6,0},{7,1},{8,14},{9,15},{10,... | collective-permute-start | bytes 393224 | tf_op jit(solution)/shard_map/ppermute | solution.py:17
  43.0 2.8 %collective-permute-done.2.refs_3_ = bf16[64,1024]{1,0:T(8,128)(2,1)S(1)} collective-permute-done((bf16[64,1024]{1,0:T(8,128)(2,1)S(1)}, bf16[64,1024]{1,0:T(8,128)(2,1)S(1)}, u32[]{:S(2)}, u32[]{:S(2)}) %collective-permute-start.2) | collective-permute-done | bytes 131104 | tf_op jit(solution)/shard_map/ppermute | solution.py:17
  45.7 4.7 %collective-permute-start.8 = (bf16[64,1024]{1,0:T(8,128)(2,1)S(1)}, bf16[64,1024]{1,0:T(8,128)(2,1)S(1)}, u32[]{:S(2)}, u32[]{:S(2)}) collective-permute-start(bf16[64,1024]{1,0:T(8,128)(2,1)S(1)} %get-tuple-element.48.refs_0_.unit_ref), channel_id=1, source_target_pairs={{0,2},{1,3},{2,0},{3,1},{4,6},{5,7},{6,4},{7,5},{8,10},{9,11},{10,... | collective-permute-start | bytes 393224 | tf_op jit(solution)/shard_map/ppermute | solution.py:17
  51.8 3.0 %collective-permute-done.8.refs_1_ = bf16[64,1024]{1,0:T(8,128)(2,1)S(1)} collective-permute-done((bf16[64,1024]{1,0:T(8,128)(2,1)S(1)}, bf16[64,1024]{1,0:T(8,128)(2,1)S(1)}, u32[]{:S(2)}, u32[]{:S(2)}) %collective-permute-start.8) | collective-permute-done | bytes 131104 | tf_op jit(solution)/shard_map/ppermute | solution.py:17
  54.7 2.8 %collective-permute-start.9 = (bf16[64,1024]{1,0:T(8,128)(2,1)S(1)}, bf16[64,1024]{1,0:T(8,128)(2,1)S(1)}, u32[]{:S(2)}, u32[]{:S(2)}) collective-permute-start(bf16[64,1024]{1,0:T(8,128)(2,1)S(1)} %get-tuple-element.48.refs_0_.unit_ref), channel_id=1, source_target_pairs={{0,4},{1,5},{2,6},{3,7},{4,0},{5,1},{6,2},{7,3},{8,12},{9,13},{10,... | collective-permute-start | bytes 393224 | tf_op jit(solution)/shard_map/ppermute | solution.py:17
  57.5 4.5 %collective-permute-done.9.refs_2_ = bf16[64,1024]{1,0:T(8,128)(2,1)S(1)} collective-permute-done((bf16[64,1024]{1,0:T(8,128)(2,1)S(1)}, bf16[64,1024]{1,0:T(8,128)(2,1)S(1)}, u32[]{:S(2)}, u32[]{:S(2)}) %collective-permute-start.9) | collective-permute-done | bytes 131104 | tf_op jit(solution)/shard_map/ppermute | solution.py:17
  63.3 2.8 %shard_map.65.refs_1_ = bf16[2048,1024]{1,0:T(8,128)(2,1)S(1)} custom-call(bf16[2048,1024]{1,0:T(8,128)(2,1)} %x_hbm.1), custom_call_target="tpu_custom_call" | custom-call | flops 16777216 | bytes 4194304 | tf_op jit(solution)/shard_map/pallas_call | solution.py:33
  66.3 1.6 %collective-permute-start.4 = (bf16[512,512]{1,0:T(8,128)(2,1)S(1)}, bf16[512,512]{1,0:T(8,128)(2,1)S(1)}, u32[]{:S(2)}, u32[]{:S(2)}) collective-permute-start(bf16[512,512]{1,0:T(8,128)(2,1)S(1)} %shard_map.58.own_ref), channel_id=1, source_target_pairs={{0,16},{8,24},{16,0},{24,8},{1,17},{9,25},{17,1},{25,9},{2,18},{10... | collective-permute-start | bytes 1572872 | tf_op jit(solution)/shard_map/ppermute | solution.py:17
  67.9 3.6 %shard_map.67.refs_3_ = f32[256,1024]{1,0:T(8,128)S(1)} custom-call(bf16[256,1024]{1,0:T(8,128)(2,1)S(1)} %shard_map.61.line_ref.refs_0_, bf16[2048,1024]{1,0:T(8,128)(2,1)S(1)} %shard_map.65.refs_1_, bf16[352,1024]{1,0:T(8,128)(2,1)S(1)} %shard_map.66.refs_2_, bf16[352,1024]{1,0:T(8,128)(2,1)S(1)} %collective-permute-done.19.refs_3_), custom_call_target="tpu_custom_call" | custom-call | flops 2885681152 | bytes 6160384 | tf_op jit(solution)/shard_map/pallas_call | solution.py:33
  75.0 1.6 %collective-permute-start.21 = (bf16[64,1024]{1,0:T(8,128)(2,1)S(1)}, bf16[64,1024]{1,0:T(8,128)(2,1)S(1)}, u32[]{:S(2)}, u32[]{:S(2)}) collective-permute-start(bf16[64,1024]{1,0:T(8,128)(2,1)S(1)} %get-tuple-element.58), channel_id=1, source_target_pairs={{0,4},{1,5},{2,6},{3,7},{4,0},{5,1},{6,2},{7,3},{8,12},{9,13},{10,... | collective-permute-start | bytes 393224 | tf_op jit(solution)/shard_map/ppermute | solution.py:17
  76.6 2.4 %collective-permute-start.22 = (bf16[64,1024]{1,0:T(8,128)(2,1)S(1)}, bf16[64,1024]{1,0:T(8,128)(2,1)S(1)}, u32[]{:S(2)}, u32[]{:S(2)}) collective-permute-start(bf16[64,1024]{1,0:T(8,128)(2,1)S(1)} %get-tuple-element.59), channel_id=1, source_target_pairs={{0,6},{1,7},{2,4},{3,5},{4,2},{5,3},{6,0},{7,1},{8,14},{9,15},{10,... | collective-permute-start | bytes 393224 | tf_op jit(solution)/shard_map/ppermute | solution.py:17
  79.7 6.8 %collective-permute-done.21.refs_5_ = bf16[64,1024]{1,0:T(8,128)(2,1)S(1)} collective-permute-done((bf16[64,1024]{1,0:T(8,128)(2,1)S(1)}, bf16[64,1024]{1,0:T(8,128)(2,1)S(1)}, u32[]{:S(2)}, u32[]{:S(2)}) %collective-permute-start.21) | collective-permute-done | bytes 131104 | tf_op jit(solution)/shard_map/ppermute | solution.py:17
  86.8 5.8 %collective-permute-start.25 = (bf16[64,512]{1,0:T(8,128)(2,1)S(1)}, bf16[64,512]{1,0:T(8,128)(2,1)S(1)}, u32[]{:S(2)}, u32[]{:S(2)}) collective-permute-start(bf16[64,512]{1,0:T(8,128)(2,1)S(1)} %get-tuple-element.60.refs_0_), channel_id=1, source_target_pairs={{0,4},{1,5},{2,6},{3,7},{4,0},{5,1},{6,2},{7,3},{8,12},{9,13},{10,... | collective-permute-start | bytes 196616 | tf_op jit(solution)/shard_map/ppermute | solution.py:17
  93.3 3.5 %collective-permute-start.26 = (bf16[64,512]{1,0:T(8,128)(2,1)S(1)}, bf16[64,512]{1,0:T(8,128)(2,1)S(1)}, u32[]{:S(2)}, u32[]{:S(2)}) collective-permute-start(bf16[64,512]{1,0:T(8,128)(2,1)S(1)} %collective-permute-done.23.refs_1_), channel_id=1, source_target_pairs={{0,4},{1,5},{2,6},{3,7},{4,0},{5,1},{6,2},{7,3},{8,12},{9,13},{10,... | collective-permute-start | bytes 196616 | tf_op jit(solution)/shard_map/ppermute | solution.py:17
  98.7 2.3 %collective-permute-start.30 = (bf16[128,512]{1,0:T(8,128)(2,1)S(1)}, bf16[128,512]{1,0:T(8,128)(2,1)S(1)}, u32[]{:S(2)}, u32[]{:S(2)}) collective-permute-start(bf16[128,512]{1,0:T(8,128)(2,1)S(1)} %shard_map.71), channel_id=1, source_target_pairs={{0,3},{1,2},{2,1},{3,0},{4,7},{5,6},{6,5},{7,4},{8,11},{9,10},{10,... | collective-permute-start | bytes 393224 | tf_op jit(solution)/shard_map/ppermute | solution.py:17
  101.2 1.8 %collective-permute-done.28.refs_6_ = bf16[64,512]{1,0:T(8,128)(2,1)S(1)} collective-permute-done((bf16[64,512]{1,0:T(8,128)(2,1)S(1)}, bf16[64,512]{1,0:T(8,128)(2,1)S(1)}, u32[]{:S(2)}, u32[]{:S(2)}) %collective-permute-start.28) | collective-permute-done | bytes 65568 | tf_op jit(solution)/shard_map/ppermute | solution.py:17
  103.1 2.2 %collective-permute-done.31.refs_9_ = bf16[64,512]{1,0:T(8,128)(2,1)S(1)} collective-permute-done((bf16[64,512]{1,0:T(8,128)(2,1)S(1)}, bf16[64,512]{1,0:T(8,128)(2,1)S(1)}, u32[]{:S(2)}, u32[]{:S(2)}) %collective-permute-start.31) | collective-permute-done | bytes 65568 | tf_op jit(solution)/shard_map/ppermute | solution.py:17
  107.5 2.1 %collective-permute-done.32.refs_10_ = bf16[64,512]{1,0:T(8,128)(2,1)S(1)} collective-permute-done((bf16[64,512]{1,0:T(8,128)(2,1)S(1)}, bf16[64,512]{1,0:T(8,128)(2,1)S(1)}, u32[]{:S(2)}, u32[]{:S(2)}) %collective-permute-start.32) | collective-permute-done | bytes 65568 | tf_op jit(solution)/shard_map/ppermute | solution.py:17
  109.6 1.9 %collective-permute-done.34.refs_12_ = bf16[64,512]{1,0:T(8,128)(2,1)S(1)} collective-permute-done((bf16[64,512]{1,0:T(8,128)(2,1)S(1)}, bf16[64,512]{1,0:T(8,128)(2,1)S(1)}, u32[]{:S(2)}, u32[]{:S(2)}) %collective-permute-start.34) | collective-permute-done | bytes 65568 | tf_op jit(solution)/shard_map/ppermute | solution.py:17
  114.9 10.7 %all_to_all.5.s_ref = f32[32,1,128]{2,1,0:T(1,128)S(1)} all-to-all(f32[32,1,128]{2,1,0:T(1,128)S(1)} %get-tuple-element.66), channel_id=1, replica_groups=mesh['gen'=4,'bank'=8] {'gen','bank'}, dimensions={0} | all-to-all | bytes 32768 | tf_op jit(solution)/shard_map/all_to_all | solution.py:535
  (64 shorter events, 19.7 us)
Async XLA Ops:
  0.0 24.6 %collective-permute-start.6 = (bf16[1024,1024]{1,0:T(8,128)(2,1)}, bf16[1024,1024]{1,0:T(8,128)(2,1)S(1)}, u32[]{:S(2)}, u32[]{:S(2)}) collective-permute-start(bf16[1024,1024]{1,0:T(8,128)(2,1)} %w_hbm.1), channel_id=1, source_target_pairs={{0,8},{8,0},{16,24},{24,16},{1,9},{9,1},{17,25},{25,17},{2,10},{10... | collective-permute-start | bytes 6291464 | tf_op jit(solution)/shard_map/ppermute | solution.py:17
  3.0 11.8 %collective-permute-start.12 = (bf16[176,1024]{1,0:T(8,128)(2,1)S(1)}, bf16[176,1024]{1,0:T(8,128)(2,1)S(1)}, u32[]{:S(2)}, u32[]{:S(2)}) collective-permute-start(bf16[176,1024]{1,0:T(8,128)(2,1)S(1)} %get-tuple-element.51), channel_id=1, source_target_pairs={{0,1},{1,0},{2,3},{3,2},{4,5},{5,4},{6,7},{7,6},{8,9},{9,8},{10,11... | collective-permute-start | bytes 1081352 | tf_op jit(solution)/shard_map/ppermute | solution.py:17
  5.6 17.0 %collective-permute-start.14 = (bf16[176,1024]{1,0:T(8,128)(2,1)S(1)}, bf16[176,1024]{1,0:T(8,128)(2,1)S(1)}, u32[]{:S(2)}, u32[]{:S(2)}) collective-permute-start(bf16[176,1024]{1,0:T(8,128)(2,1)S(1)} %get-tuple-element.52), channel_id=1, source_target_pairs={{0,1},{1,0},{2,3},{3,2},{4,5},{5,4},{6,7},{7,6},{8,9},{9,8},{10,11... | collective-permute-start | bytes 1081352 | tf_op jit(solution)/shard_map/ppermute | solution.py:17
  5.7 12.8 %collective-permute-start.5 = (bf16[64,2048]{1,0:T(8,128)(2,1)S(1)}, bf16[64,2048]{1,0:T(8,128)(2,1)S(1)}, u32[]{:S(2)}, u32[]{:S(2)}) collective-permute-start(bf16[64,2048]{1,0:T(8,128)(2,1)S(1)} %get-tuple-element.43), channel_id=1, source_target_pairs={{0,16},{8,24},{16,0},{24,8},{1,17},{9,25},{17,1},{25,9},{2,18},{10... | collective-permute-start | bytes 786440 | tf_op jit(solution)/shard_map/ppermute | solution.py:17
  7.6 34.8 %collective-permute-start.17 = (bf16[320,1024]{1,0:T(8,128)(2,1)S(1)}, bf16[320,1024]{1,0:T(8,128)(2,1)S(1)}, u32[]{:S(2)}, u32[]{:S(2)}) collective-permute-start(bf16[320,1024]{1,0:T(8,128)(2,1)S(1)} %get-tuple-element.53), channel_id=1, source_target_pairs={{0,1},{1,0},{2,3},{3,2},{4,5},{5,4},{6,7},{7,6},{8,9},{9,8},{10,11... | collective-permute-start | bytes 1966088 | tf_op jit(solution)/shard_map/ppermute | solution.py:17
  14.9 10.7 %collective-permute-start.13 = (bf16[176,1024]{1,0:T(8,128)(2,1)S(1)}, bf16[176,1024]{1,0:T(8,128)(2,1)S(1)}, u32[]{:S(2)}, u32[]{:S(2)}) collective-permute-start(bf16[176,1024]{1,0:T(8,128)(2,1)S(1)} %collective-permute-done.12.refs_0_), channel_id=1, source_target_pairs={{0,16},{8,24},{16,0},{24,8},{1,17},{9,25},{17,1},{25,9},{2,18},{10... | collective-permute-start | bytes 1081352 | tf_op jit(solution)/shard_map/ppermute | solution.py:17
  18.5 7.0 %collective-permute-start = (bf16[64,1024]{1,0:T(8,128)(2,1)S(1)}, bf16[64,1024]{1,0:T(8,128)(2,1)S(1)}, u32[]{:S(2)}, u32[]{:S(2)}) collective-permute-start(bf16[64,1024]{1,0:T(8,128)(2,1)S(1)} %get-tuple-element.38), channel_id=1, source_target_pairs={{0,2},{1,3},{2,0},{3,1},{4,6},{5,7},{6,4},{7,5},{8,10},{9,11},{10,... | collective-permute-start | bytes 393224 | tf_op jit(solution)/shard_map/ppermute | solution.py:17
  22.6 19.4 %collective-permute-start.15 = (bf16[176,1024]{1,0:T(8,128)(2,1)S(1)}, bf16[176,1024]{1,0:T(8,128)(2,1)S(1)}, u32[]{:S(2)}, u32[]{:S(2)}) collective-permute-start(bf16[176,1024]{1,0:T(8,128)(2,1)S(1)} %collective-permute-done.14.refs_1_), channel_id=1, source_target_pairs={{0,16},{8,24},{16,0},{24,8},{1,17},{9,25},{17,1},{25,9},{2,18},{10... | collective-permute-start | bytes 1081352 | tf_op jit(solution)/shard_map/ppermute | solution.py:17
  24.7 43.2 %collective-permute-start.19 = (bf16[352,1024]{1,0:T(8,128)(2,1)S(1)}, bf16[352,1024]{1,0:T(8,128)(2,1)S(1)}, u32[]{:S(2)}, u32[]{:S(2)}) collective-permute-start(bf16[352,1024]{1,0:T(8,128)(2,1)S(1)} %shard_map.66.refs_2_), channel_id=1, source_target_pairs={{0,8},{8,0},{16,24},{24,16},{1,9},{9,1},{17,25},{25,17},{2,10},{10... | collective-permute-start | bytes 2162696 | tf_op jit(solution)/shard_map/ppermute | solution.py:17
  25.5 12.8 %collective-permute-start.7 = (f32[64,1024]{1,0:T(8,128)S(1)}, f32[64,1024]{1,0:T(8,128)S(1)}, u32[]{:S(2)}, u32[]{:S(2)}) collective-permute-start(f32[64,1024]{1,0:T(8,128)S(1)} %get-tuple-element.47), channel_id=1, source_target_pairs={{0,16},{8,24},{16,0},{24,8},{1,17},{9,25},{17,1},{25,9},{2,18},{10... | collective-permute-start | bytes 786440 | tf_op jit(solution)/shard_map/ppermute | solution.py:17
  25.6 16.8 %collective-permute-start.1 = (bf16[64,1024]{1,0:T(8,128)(2,1)S(1)}, bf16[64,1024]{1,0:T(8,128)(2,1)S(1)}, u32[]{:S(2)}, u32[]{:S(2)}) collective-permute-start(bf16[64,1024]{1,0:T(8,128)(2,1)S(1)} %get-tuple-element.39), channel_id=1, source_target_pairs={{0,4},{1,5},{2,6},{3,7},{4,0},{5,1},{6,2},{7,3},{8,12},{9,13},{10,... | collective-permute-start | bytes 393224 | tf_op jit(solution)/shard_map/ppermute | solution.py:17
  38.3 7.5 %collective-permute-start.2 = (bf16[64,1024]{1,0:T(8,128)(2,1)S(1)}, bf16[64,1024]{1,0:T(8,128)(2,1)S(1)}, u32[]{:S(2)}, u32[]{:S(2)}) collective-permute-start(bf16[64,1024]{1,0:T(8,128)(2,1)S(1)} %get-tuple-element.40), channel_id=1, source_target_pairs={{0,6},{1,7},{2,4},{3,5},{4,2},{5,3},{6,0},{7,1},{8,14},{9,15},{10,... | collective-permute-start | bytes 393224 | tf_op jit(solution)/shard_map/ppermute | solution.py:17
  42.0 8.6 %collective-permute-start.10 = (bf16[64,1024]{1,0:T(8,128)(2,1)S(1)}, bf16[64,1024]{1,0:T(8,128)(2,1)S(1)}, u32[]{:S(2)}, u32[]{:S(2)}) collective-permute-start(bf16[64,1024]{1,0:T(8,128)(2,1)S(1)} %get-tuple-element.48.refs_0_.unit_ref), channel_id=1, source_target_pairs={{0,6},{1,7},{2,4},{3,5},{4,2},{5,3},{6,0},{7,1},{8,14},{9,15},{10,... | collective-permute-start | bytes 393224 | tf_op jit(solution)/shard_map/ppermute | solution.py:17
  42.4 30.7 %collective-permute-start.16 = (bf16[352,1024]{1,0:T(8,128)(2,1)S(1)}, bf16[352,1024]{1,0:T(8,128)(2,1)S(1)}, u32[]{:S(2)}, u32[]{:S(2)}) collective-permute-start(bf16[352,1024]{1,0:T(8,128)(2,1)S(1)} %shard_map.64.refs_1_), channel_id=1, source_target_pairs={{0,8},{8,0},{16,24},{24,16},{1,9},{9,1},{17,25},{25,17},{2,10},{10... | collective-permute-start | bytes 2162696 | tf_op jit(solution)/shard_map/ppermute | solution.py:17
  42.5 30.6 %collective-permute-start.18 = (bf16[320,1024]{1,0:T(8,128)(2,1)S(1)}, bf16[320,1024]{1,0:T(8,128)(2,1)S(1)}, u32[]{:S(2)}, u32[]{:S(2)}) collective-permute-start(bf16[320,1024]{1,0:T(8,128)(2,1)S(1)} %collective-permute-done.17.refs_2_), channel_id=1, source_target_pairs={{0,8},{8,0},{16,24},{24,16},{1,9},{9,1},{17,25},{25,17},{2,10},{10... | collective-permute-start | bytes 1966088 | tf_op jit(solution)/shard_map/ppermute | solution.py:17
  45.7 9.0 %collective-permute-start.8 = (bf16[64,1024]{1,0:T(8,128)(2,1)S(1)}, bf16[64,1024]{1,0:T(8,128)(2,1)S(1)}, u32[]{:S(2)}, u32[]{:S(2)}) collective-permute-start(bf16[64,1024]{1,0:T(8,128)(2,1)S(1)} %get-tuple-element.48.refs_0_.unit_ref), channel_id=1, source_target_pairs={{0,2},{1,3},{2,0},{3,1},{4,6},{5,7},{6,4},{7,5},{8,10},{9,11},{10,... | collective-permute-start | bytes 393224 | tf_op jit(solution)/shard_map/ppermute | solution.py:17
  50.5 15.6 %collective-permute-start.3 = (bf16[256,512]{1,0:T(8,128)(2,1)S(1)}, bf16[256,512]{1,0:T(8,128)(2,1)S(1)}, u32[]{:S(2)}, u32[]{:S(2)}) collective-permute-start(bf16[256,512]{1,0:T(8,128)(2,1)S(1)} %get-tuple-element.42), channel_id=1, source_target_pairs={{0,1},{1,0},{2,3},{3,2},{4,5},{5,4},{6,7},{7,6},{8,9},{9,8},{10,11... | collective-permute-start | bytes 786440 | tf_op jit(solution)/shard_map/ppermute | solution.py:17
  54.7 7.3 %collective-permute-start.9 = (bf16[64,1024]{1,0:T(8,128)(2,1)S(1)}, bf16[64,1024]{1,0:T(8,128)(2,1)S(1)}, u32[]{:S(2)}, u32[]{:S(2)}) collective-permute-start(bf16[64,1024]{1,0:T(8,128)(2,1)S(1)} %get-tuple-element.48.refs_0_.unit_ref), channel_id=1, source_target_pairs={{0,4},{1,5},{2,6},{3,7},{4,0},{5,1},{6,2},{7,3},{8,12},{9,13},{10,... | collective-permute-start | bytes 393224 | tf_op jit(solution)/shard_map/ppermute | solution.py:17
  62.0 16.9 %collective-permute-start.11 = (bf16[256,1024]{1,0:T(8,128)(2,1)S(1)}, bf16[256,1024]{1,0:T(8,128)(2,1)S(1)}, u32[]{:S(2)}, u32[]{:S(2)}) collective-permute-start(bf16[256,1024]{1,0:T(8,128)(2,1)S(1)} %shard_map.61.line_ref.refs_0_), channel_id=1, source_target_pairs={{0,1},{1,0},{2,3},{3,2},{4,5},{5,4},{6,7},{7,6},{8,9},{9,8},{10,11... | collective-permute-start | bytes 1572872 | tf_op jit(solution)/shard_map/ppermute | solution.py:17
  66.3 31.2 %collective-permute-start.4 = (bf16[512,512]{1,0:T(8,128)(2,1)S(1)}, bf16[512,512]{1,0:T(8,128)(2,1)S(1)}, u32[]{:S(2)}, u32[]{:S(2)}) collective-permute-start(bf16[512,512]{1,0:T(8,128)(2,1)S(1)} %shard_map.58.own_ref), channel_id=1, source_target_pairs={{0,16},{8,24},{16,0},{24,8},{1,17},{9,25},{17,1},{25,9},{2,18},{10... | collective-permute-start | bytes 1572872 | tf_op jit(solution)/shard_map/ppermute | solution.py:17
  74.5 5.2 %collective-permute-start.20 = (bf16[64,1024]{1,0:T(8,128)(2,1)S(1)}, bf16[64,1024]{1,0:T(8,128)(2,1)S(1)}, u32[]{:S(2)}, u32[]{:S(2)}) collective-permute-start(bf16[64,1024]{1,0:T(8,128)(2,1)S(1)} %get-tuple-element.57), channel_id=1, source_target_pairs={{0,2},{1,3},{2,0},{3,1},{4,6},{5,7},{6,4},{7,5},{8,10},{9,11},{10,... | collective-permute-start | bytes 393224 | tf_op jit(solution)/shard_map/ppermute | solution.py:17
  75.0 11.5 %collective-permute-start.21 = (bf16[64,1024]{1,0:T(8,128)(2,1)S(1)}, bf16[64,1024]{1,0:T(8,128)(2,1)S(1)}, u32[]{:S(2)}, u32[]{:S(2)}) collective-permute-start(bf16[64,1024]{1,0:T(8,128)(2,1)S(1)} %get-tuple-element.58), channel_id=1, source_target_pairs={{0,4},{1,5},{2,6},{3,7},{4,0},{5,1},{6,2},{7,3},{8,12},{9,13},{10,... | collective-permute-start | bytes 393224 | tf_op jit(solution)/shard_map/ppermute | solution.py:17
  76.6 9.9 %collective-permute-start.22 = (bf16[64,1024]{1,0:T(8,128)(2,1)S(1)}, bf16[64,1024]{1,0:T(8,128)(2,1)S(1)}, u32[]{:S(2)}, u32[]{:S(2)}) collective-permute-start(bf16[64,1024]{1,0:T(8,128)(2,1)S(1)} %get-tuple-element.59), channel_id=1, source_target_pairs={{0,6},{1,7},{2,4},{3,5},{4,2},{5,3},{6,0},{7,1},{8,14},{9,15},{10,... | collective-permute-start | bytes 393224 | tf_op jit(solution)/shard_map/ppermute | solution.py:17
  86.7 6.6 %collective-permute-start.23 = (bf16[64,512]{1,0:T(8,128)(2,1)S(1)}, bf16[64,512]{1,0:T(8,128)(2,1)S(1)}, u32[]{:S(2)}, u32[]{:S(2)}) collective-permute-start(bf16[64,512]{1,0:T(8,128)(2,1)S(1)} %get-tuple-element.61), channel_id=1, source_target_pairs={{0,16},{8,24},{16,0},{24,8},{1,17},{9,25},{17,1},{25,9},{2,18},{10... | collective-permute-start | bytes 196616 | tf_op jit(solution)/shard_map/ppermute | solution.py:17
  86.8 10.8 %collective-permute-start.25 = (bf16[64,512]{1,0:T(8,128)(2,1)S(1)}, bf16[64,512]{1,0:T(8,128)(2,1)S(1)}, u32[]{:S(2)}, u32[]{:S(2)}) collective-permute-start(bf16[64,512]{1,0:T(8,128)(2,1)S(1)} %get-tuple-element.60.refs_0_), channel_id=1, source_target_pairs={{0,4},{1,5},{2,6},{3,7},{4,0},{5,1},{6,2},{7,3},{8,12},{9,13},{10,... | collective-permute-start | bytes 196616 | tf_op jit(solution)/shard_map/ppermute | solution.py:17
  92.6 6.1 %collective-permute-start.27 = (bf16[64,512]{1,0:T(8,128)(2,1)S(1)}, bf16[64,512]{1,0:T(8,128)(2,1)S(1)}, u32[]{:S(2)}, u32[]{:S(2)}) collective-permute-start(bf16[64,512]{1,0:T(8,128)(2,1)S(1)} %get-tuple-element.60.refs_0_), channel_id=1, source_target_pairs={{0,6},{1,7},{2,4},{3,5},{4,2},{5,3},{6,0},{7,1},{8,14},{9,15},{10,... | collective-permute-start | bytes 196616 | tf_op jit(solution)/shard_map/ppermute | solution.py:17
  93.3 7.7 %collective-permute-start.26 = (bf16[64,512]{1,0:T(8,128)(2,1)S(1)}, bf16[64,512]{1,0:T(8,128)(2,1)S(1)}, u32[]{:S(2)}, u32[]{:S(2)}) collective-permute-start(bf16[64,512]{1,0:T(8,128)(2,1)S(1)} %collective-permute-done.23.refs_1_), channel_id=1, source_target_pairs={{0,4},{1,5},{2,6},{3,7},{4,0},{5,1},{6,2},{7,3},{8,12},{9,13},{10,... | collective-permute-start | bytes 196616 | tf_op jit(solution)/shard_map/ppermute | solution.py:17
  96.8 6.2 %collective-permute-start.28 = (bf16[64,512]{1,0:T(8,128)(2,1)S(1)}, bf16[64,512]{1,0:T(8,128)(2,1)S(1)}, u32[]{:S(2)}, u32[]{:S(2)}) collective-permute-start(bf16[64,512]{1,0:T(8,128)(2,1)S(1)} %collective-permute-done.23.refs_1_), channel_id=1, source_target_pairs={{0,6},{1,7},{2,4},{3,5},{4,2},{5,3},{6,0},{7,1},{8,14},{9,15},{10,... | collective-permute-start | bytes 196616 | tf_op jit(solution)/shard_map/ppermute | solution.py:17
  97.5 10.0 %collective-permute-start.24 = (bf16[128,512]{1,0:T(8,128)(2,1)S(1)}, bf16[128,512]{1,0:T(8,128)(2,1)S(1)}, u32[]{:S(2)}, u32[]{:S(2)}) collective-permute-start(bf16[128,512]{1,0:T(8,128)(2,1)S(1)} %shard_map.71), channel_id=1, source_target_pairs={{0,2},{1,3},{2,0},{3,1},{4,6},{5,7},{6,4},{7,5},{8,10},{9,11},{10,... | collective-permute-start | bytes 393224 | tf_op jit(solution)/shard_map/ppermute | solution.py:17
  97.6 9.9 %collective-permute-start.29 = (bf16[128,512]{1,0:T(8,128)(2,1)S(1)}, bf16[128,512]{1,0:T(8,128)(2,1)S(1)}, u32[]{:S(2)}, u32[]{:S(2)}) collective-permute-start(bf16[128,512]{1,0:T(8,128)(2,1)S(1)} %shard_map.71), channel_id=1, source_target_pairs={{0,1},{1,0},{2,3},{3,2},{4,5},{5,4},{6,7},{7,6},{8,9},{9,8},{10,11... | collective-permute-start | bytes 393224 | tf_op jit(solution)/shard_map/ppermute | solution.py:17
  98.7 8.8 %collective-permute-start.30 = (bf16[128,512]{1,0:T(8,128)(2,1)S(1)}, bf16[128,512]{1,0:T(8,128)(2,1)S(1)}, u32[]{:S(2)}, u32[]{:S(2)}) collective-permute-start(bf16[128,512]{1,0:T(8,128)(2,1)S(1)} %shard_map.71), channel_id=1, source_target_pairs={{0,3},{1,2},{2,1},{3,0},{4,7},{5,6},{6,5},{7,4},{8,11},{9,10},{10,... | collective-permute-start | bytes 393224 | tf_op jit(solution)/shard_map/ppermute | solution.py:17
  114.0 11.6 %collective-permute-start.36 = (f32[128,512]{1,0:T(8,128)S(1)}, f32[128,512]{1,0:T(8,128)S(1)}, u32[]{:S(2)}, u32[]{:S(2)}) collective-permute-start(f32[128,512]{1,0:T(8,128)S(1)} %get-tuple-element.65), channel_id=1, source_target_pairs={{0,16},{8,24},{16,0},{24,8},{1,17},{9,25},{17,1},{25,9},{2,18},{10... | collective-permute-start | bytes 786440 | tf_op jit(solution)/shard_map/ppermute | solution.py:17
  (5 other events, 19.0 us)
where the time goes:
time: 127 us
  starting transfers between devices  52 us (41%)
  waiting for transfers between devices  45.8 us (36%)
  Pallas kernels  17.7 us (14%)
  blocking collectives  10.7 us (8%)
    ppermute x37, starting transfers between devices, swap(): return lax.ppermute(value, axis, [(i, i ^ mask) for i in range(count)])  52 us
    ppermute x37, waiting for transfers between devices, swap(): return lax.ppermute(value, axis, [(i, i ^ mask) for i in range(count)])  45.8 us
    pallas_call x21, Pallas kernels, call(): pl.pallas_call(body, in_specs=[HBM if there else VMEM for there in far_aw...  17.7 us
    all_to_all x1, blocking collectives, local(): squares = lax.all_to_all(squares, (GEN, BANK), 0, 0, tiled=True)  10.7 us
  transfers between devices with their start and end apart: 37, of which 14 were waited for; matrix products, arithmetic and copies ran while one was open for 0% of the time, Pallas kernels for 13%

commit v1 on v0

--- a/solution.py
+++ b/solution.py
@@ -382,16 +382,17 @@
         for side in (0, 1):
             start = 2 * (place[0] ^ side) + (place[1] ^ core)
             start = pl.multiple_of(start * piece, piece)
-            outs[0][side * piece : (side + 1) * piece] = jnp.dot(
+            total = jnp.dot(
                 own_ref[pl.ds(start, piece), :], held[:batch], preferred_element_type=F32
             ) + jnp.dot(
                 other_ref[pl.ds(start, piece), :], held[batch:], preferred_element_type=F32
             )
+            outs[0][side * piece : (side + 1) * piece] = total.astype(outs[0].dtype)
 
     return call(
         body,
         list(columns) + arrays,
-        [((2 * piece, width), F32)] + [((2 * batch, width), BF16)] * fresh,
+        [((2 * piece, width), BF16 if core else F32)] + [((2 * batch, width), BF16)] * fresh,
         8 * piece * width * batch,
     )
 
@@ -402,7 +403,7 @@
     def body(a_ref, b_ref, home_ref, away_ref, out_ref):
         total = 0.0
         for ref, at in ((home_ref, slice(0, rows)), (away_ref, slice(rows, 2 * rows))):
-            block = a_ref[at] + b_ref[at]
+            block = a_ref[at] + b_ref[at].astype(F32)
             ref[...] = block
             total = total + jnp.sum((block * block).reshape(rows // 8, 8, width), axis=0)
         tile = total[:, :128]

time: 127 us -> 126 us (level)
  no operation moved by 1% of the time
where the time goes in v1:
time: 126 us
  starting transfers between devices  52 us (41%)
  waiting for transfers between devices  45.5 us (36%)
  Pallas kernels  17.7 us (14%)
  blocking collectives  10.7 us (8%)
    ppermute x37, starting transfers between devices, swap(): return lax.ppermute(value, axis, [(i, i ^ mask) for i in range(count)])  52 us
    ppermute x37, waiting for transfers between devices, swap(): return lax.ppermute(value, axis, [(i, i ^ mask) for i in range(count)])  45.5 us
    pallas_call x21, Pallas kernels, call(): pl.pallas_call(body, in_specs=[HBM if there else VMEM for there in far_aw...  17.7 us
    all_to_all x1, blocking collectives, local(): squares = lax.all_to_all(squares, (GEN, BANK), 0, 0, tiled=True)  10.7 us
  transfers between devices with their start and end apart: 37, of which 14 were waited for; matrix products, arithmetic and copies ran while one was open for 0% of the time, Pallas kernels for 13%

profile of v1, /device:TPU:0, one launch (start us, length us, event | category | flops | bytes accessed | tf_op | source)
XLA Modules:
  0.0 126.2 jit_solution(6573250600601086180)
XLA Ops:
  0.5 2.0 %shard_map.55 = (bf16[64,4096]{1,0:T(8,128)(2,1)S(1)}, bf16[64,2048]{1,0:T(8,128)(2,1)S(1)}, bf16[64,2048]{1,0:T(8,128)(2,1)S(1)}, bf16[352,1024]{1,0:T(8,128)(2,1)S(1)}, bf16[320,1024]{1,0:T(8,128)(2,1)S(1)}) custom-call(bf16[64,4096]{1,0:T(8,128)(2,1)} %refs_0_.1, bf16[64,4096]{1,0:T(8,128)(2,1)} %refs_1_.1, bf16[64,4096]{1,0:T(8,128)(2,1)} %refs_2_.1, ...), custom_call_target="tpu_custom_call" | custom-call | flops 2097152 | bytes 5767168 | tf_op jit(solution)/shard_map/pallas_call | solution.py:33
  3.0 2.6 %collective-permute-start.12 = (bf16[176,1024]{1,0:T(8,128)(2,1)S(1)}, bf16[176,1024]{1,0:T(8,128)(2,1)S(1)}, u32[]{:S(2)}, u32[]{:S(2)}) collective-permute-start(bf16[176,1024]{1,0:T(8,128)(2,1)S(1)} %get-tuple-element.51), channel_id=1, source_target_pairs={{0,1},{1,0},{2,3},{3,2},{4,5},{5,4},{6,7},{7,6},{8,9},{9,8},{10,11... | collective-permute-start | bytes 1081352 | tf_op jit(solution)/shard_map/ppermute | solution.py:17
  5.7 1.9 %collective-permute-start.5 = (bf16[64,2048]{1,0:T(8,128)(2,1)S(1)}, bf16[64,2048]{1,0:T(8,128)(2,1)S(1)}, u32[]{:S(2)}, u32[]{:S(2)}) collective-permute-start(bf16[64,2048]{1,0:T(8,128)(2,1)S(1)} %get-tuple-element.43), channel_id=1, source_target_pairs={{0,16},{8,24},{16,0},{24,8},{1,17},{9,25},{17,1},{25,9},{2,18},{10... | collective-permute-start | bytes 786440 | tf_op jit(solution)/shard_map/ppermute | solution.py:17
  7.6 1.5 %collective-permute-start.17 = (bf16[320,1024]{1,0:T(8,128)(2,1)S(1)}, bf16[320,1024]{1,0:T(8,128)(2,1)S(1)}, u32[]{:S(2)}, u32[]{:S(2)}) collective-permute-start(bf16[320,1024]{1,0:T(8,128)(2,1)S(1)} %get-tuple-element.53), channel_id=1, source_target_pairs={{0,1},{1,0},{2,3},{3,2},{4,5},{5,4},{6,7},{7,6},{8,9},{9,8},{10,11... | collective-permute-start | bytes 1966088 | tf_op jit(solution)/shard_map/ppermute | solution.py:17
  9.1 5.7 %collective-permute-done.12.refs_0_ = bf16[176,1024]{1,0:T(8,128)(2,1)S(1)} collective-permute-done((bf16[176,1024]{1,0:T(8,128)(2,1)S(1)}, bf16[176,1024]{1,0:T(8,128)(2,1)S(1)}, u32[]{:S(2)}, u32[]{:S(2)}) %collective-permute-start.12) | collective-permute-done | bytes 360480 | tf_op jit(solution)/shard_map/ppermute | solution.py:17
  14.9 2.0 %collective-permute-start.13 = (bf16[176,1024]{1,0:T(8,128)(2,1)S(1)}, bf16[176,1024]{1,0:T(8,128)(2,1)S(1)}, u32[]{:S(2)}, u32[]{:S(2)}) collective-permute-start(bf16[176,1024]{1,0:T(8,128)(2,1)S(1)} %collective-permute-done.12.refs_0_), channel_id=1, source_target_pairs={{0,16},{8,24},{16,0},{24,8},{1,17},{9,25},{17,1},{25,9},{2,18},{10... | collective-permute-start | bytes 1081352 | tf_op jit(solution)/shard_map/ppermute | solution.py:17
  16.9 1.6 %shard_map.56 = (bf16[1024,1024]{1,0:T(8,128)(2,1)S(1)}, bf16[64,1024]{1,0:T(8,128)(2,1)S(1)}, bf16[64,1024]{1,0:T(8,128)(2,1)S(1)}, bf16[64,1024]{1,0:T(8,128)(2,1)S(1)}, bf16[64,1024]{1,0:T(8,128)(2,1)S(1)}) custom-call(bf16[64,4096]{1,0:T(8,128)(2,1)S(1)} %get-tuple-element.36.hid_ref, bf16[1024,1024]{1,0:T(8,128)(2,1)} %w_hbm.1), custom_call_target="tpu_custom_call" | custom-call | bytes 2621440 | tf_op jit(solution)/shard_map/pallas_call | solution.py:33
  18.5 1.6 %collective-permute-start = (bf16[64,1024]{1,0:T(8,128)(2,1)S(1)}, bf16[64,1024]{1,0:T(8,128)(2,1)S(1)}, u32[]{:S(2)}, u32[]{:S(2)}) collective-permute-start(bf16[64,1024]{1,0:T(8,128)(2,1)S(1)} %get-tuple-element.38), channel_id=1, source_target_pairs={{0,2},{1,3},{2,0},{3,1},{4,6},{5,7},{6,4},{7,5},{8,10},{9,11},{10,... | collective-permute-start | bytes 393224 | tf_op jit(solution)/shard_map/ppermute | solution.py:17
  20.1 2.5 %collective-permute-done.14.refs_1_ = bf16[176,1024]{1,0:T(8,128)(2,1)S(1)} collective-permute-done((bf16[176,1024]{1,0:T(8,128)(2,1)S(1)}, bf16[176,1024]{1,0:T(8,128)(2,1)S(1)}, u32[]{:S(2)}, u32[]{:S(2)}) %collective-permute-start.14) | collective-permute-done | bytes 360480 | tf_op jit(solution)/shard_map/ppermute | solution.py:17
  22.6 2.0 %collective-permute-start.15 = (bf16[176,1024]{1,0:T(8,128)(2,1)S(1)}, bf16[176,1024]{1,0:T(8,128)(2,1)S(1)}, u32[]{:S(2)}, u32[]{:S(2)}) collective-permute-start(bf16[176,1024]{1,0:T(8,128)(2,1)S(1)} %collective-permute-done.14.refs_1_), channel_id=1, source_target_pairs={{0,16},{8,24},{16,0},{24,8},{1,17},{9,25},{17,1},{25,9},{2,18},{10... | collective-permute-start | bytes 1081352 | tf_op jit(solution)/shard_map/ppermute | solution.py:17
  25.6 3.1 %collective-permute-start.1 = (bf16[64,1024]{1,0:T(8,128)(2,1)S(1)}, bf16[64,1024]{1,0:T(8,128)(2,1)S(1)}, u32[]{:S(2)}, u32[]{:S(2)}) collective-permute-start(bf16[64,1024]{1,0:T(8,128)(2,1)S(1)} %get-tuple-element.39), channel_id=1, source_target_pairs={{0,4},{1,5},{2,6},{3,7},{4,0},{5,1},{6,2},{7,3},{8,12},{9,13},{10,... | collective-permute-start | bytes 393224 | tf_op jit(solution)/shard_map/ppermute | solution.py:17
  28.7 9.6 %collective-permute-done.7.b_ref = f32[64,1024]{1,0:T(8,128)S(1)} collective-permute-done((f32[64,1024]{1,0:T(8,128)S(1)}, f32[64,1024]{1,0:T(8,128)S(1)}, u32[]{:S(2)}, u32[]{:S(2)}) %collective-permute-start.7) | collective-permute-done | bytes 262176 | tf_op jit(solution)/shard_map/ppermute | solution.py:17
  38.3 3.5 %collective-permute-start.2 = (bf16[64,1024]{1,0:T(8,128)(2,1)S(1)}, bf16[64,1024]{1,0:T(8,128)(2,1)S(1)}, u32[]{:S(2)}, u32[]{:S(2)}) collective-permute-start(bf16[64,1024]{1,0:T(8,128)(2,1)S(1)} %get-tuple-element.40), channel_id=1, source_target_pairs={{0,6},{1,7},{2,4},{3,5},{4,2},{5,3},{6,0},{7,1},{8,14},{9,15},{10,... | collective-permute-start | bytes 393224 | tf_op jit(solution)/shard_map/ppermute | solution.py:17
  43.0 2.8 %collective-permute-done.2.refs_3_ = bf16[64,1024]{1,0:T(8,128)(2,1)S(1)} collective-permute-done((bf16[64,1024]{1,0:T(8,128)(2,1)S(1)}, bf16[64,1024]{1,0:T(8,128)(2,1)S(1)}, u32[]{:S(2)}, u32[]{:S(2)}) %collective-permute-start.2) | collective-permute-done | bytes 131104 | tf_op jit(solution)/shard_map/ppermute | solution.py:17
  45.7 4.7 %collective-permute-start.8 = (bf16[64,1024]{1,0:T(8,128)(2,1)S(1)}, bf16[64,1024]{1,0:T(8,128)(2,1)S(1)}, u32[]{:S(2)}, u32[]{:S(2)}) collective-permute-start(bf16[64,1024]{1,0:T(8,128)(2,1)S(1)} %get-tuple-element.48.refs_0_.unit_ref), channel_id=1, source_target_pairs={{0,2},{1,3},{2,0},{3,1},{4,6},{5,7},{6,4},{7,5},{8,10},{9,11},{10,... | collective-permute-start | bytes 393224 | tf_op jit(solution)/shard_map/ppermute | solution.py:17
  51.8 3.0 %collective-permute-done.8.refs_1_ = bf16[64,1024]{1,0:T(8,128)(2,1)S(1)} collective-permute-done((bf16[64,1024]{1,0:T(8,128)(2,1)S(1)}, bf16[64,1024]{1,0:T(8,128)(2,1)S(1)}, u32[]{:S(2)}, u32[]{:S(2)}) %collective-permute-start.8) | collective-permute-done | bytes 131104 | tf_op jit(solution)/shard_map/ppermute | solution.py:17
  54.7 2.8 %collective-permute-start.9 = (bf16[64,1024]{1,0:T(8,128)(2,1)S(1)}, bf16[64,1024]{1,0:T(8,128)(2,1)S(1)}, u32[]{:S(2)}, u32[]{:S(2)}) collective-permute-start(bf16[64,1024]{1,0:T(8,128)(2,1)S(1)} %get-tuple-element.48.refs_0_.unit_ref), channel_id=1, source_target_pairs={{0,4},{1,5},{2,6},{3,7},{4,0},{5,1},{6,2},{7,3},{8,12},{9,13},{10,... | collective-permute-start | bytes 393224 | tf_op jit(solution)/shard_map/ppermute | solution.py:17
  57.5 4.5 %collective-permute-done.9.refs_2_ = bf16[64,1024]{1,0:T(8,128)(2,1)S(1)} collective-permute-done((bf16[64,1024]{1,0:T(8,128)(2,1)S(1)}, bf16[64,1024]{1,0:T(8,128)(2,1)S(1)}, u32[]{:S(2)}, u32[]{:S(2)}) %collective-permute-start.9) | collective-permute-done | bytes 131104 | tf_op jit(solution)/shard_map/ppermute | solution.py:17
  63.3 2.8 %shard_map.65.refs_1_ = bf16[2048,1024]{1,0:T(8,128)(2,1)S(1)} custom-call(bf16[2048,1024]{1,0:T(8,128)(2,1)} %x_hbm.1), custom_call_target="tpu_custom_call" | custom-call | flops 16777216 | bytes 4194304 | tf_op jit(solution)/shard_map/pallas_call | solution.py:33
  66.3 1.6 %collective-permute-start.4 = (bf16[512,512]{1,0:T(8,128)(2,1)S(1)}, bf16[512,512]{1,0:T(8,128)(2,1)S(1)}, u32[]{:S(2)}, u32[]{:S(2)}) collective-permute-start(bf16[512,512]{1,0:T(8,128)(2,1)S(1)} %shard_map.58.own_ref), channel_id=1, source_target_pairs={{0,16},{8,24},{16,0},{24,8},{1,17},{9,25},{17,1},{25,9},{2,18},{10... | collective-permute-start | bytes 1572872 | tf_op jit(solution)/shard_map/ppermute | solution.py:17
  67.9 3.6 %shard_map.67.refs_3_ = f32[256,1024]{1,0:T(8,128)S(1)} custom-call(bf16[256,1024]{1,0:T(8,128)(2,1)S(1)} %shard_map.61.line_ref.refs_0_, bf16[2048,1024]{1,0:T(8,128)(2,1)S(1)} %shard_map.65.refs_1_, bf16[352,1024]{1,0:T(8,128)(2,1)S(1)} %shard_map.66.refs_2_, bf16[352,1024]{1,0:T(8,128)(2,1)S(1)} %collective-permute-done.19.refs_3_), custom_call_target="tpu_custom_call" | custom-call | flops 2885681152 | bytes 6160384 | tf_op jit(solution)/shard_map/pallas_call | solution.py:33
  75.0 1.6 %collective-permute-start.21 = (bf16[64,1024]{1,0:T(8,128)(2,1)S(1)}, bf16[64,1024]{1,0:T(8,128)(2,1)S(1)}, u32[]{:S(2)}, u32[]{:S(2)}) collective-permute-start(bf16[64,1024]{1,0:T(8,128)(2,1)S(1)} %get-tuple-element.58), channel_id=1, source_target_pairs={{0,4},{1,5},{2,6},{3,7},{4,0},{5,1},{6,2},{7,3},{8,12},{9,13},{10,... | collective-permute-start | bytes 393224 | tf_op jit(solution)/shard_map/ppermute | solution.py:17
  76.6 2.4 %collective-permute-start.22 = (bf16[64,1024]{1,0:T(8,128)(2,1)S(1)}, bf16[64,1024]{1,0:T(8,128)(2,1)S(1)}, u32[]{:S(2)}, u32[]{:S(2)}) collective-permute-start(bf16[64,1024]{1,0:T(8,128)(2,1)S(1)} %get-tuple-element.59), channel_id=1, source_target_pairs={{0,6},{1,7},{2,4},{3,5},{4,2},{5,3},{6,0},{7,1},{8,14},{9,15},{10,... | collective-permute-start | bytes 393224 | tf_op jit(solution)/shard_map/ppermute | solution.py:17
  79.7 6.8 %collective-permute-done.21.refs_5_ = bf16[64,1024]{1,0:T(8,128)(2,1)S(1)} collective-permute-done((bf16[64,1024]{1,0:T(8,128)(2,1)S(1)}, bf16[64,1024]{1,0:T(8,128)(2,1)S(1)}, u32[]{:S(2)}, u32[]{:S(2)}) %collective-permute-start.21) | collective-permute-done | bytes 131104 | tf_op jit(solution)/shard_map/ppermute | solution.py:17
  86.8 5.8 %collective-permute-start.25 = (bf16[64,512]{1,0:T(8,128)(2,1)S(1)}, bf16[64,512]{1,0:T(8,128)(2,1)S(1)}, u32[]{:S(2)}, u32[]{:S(2)}) collective-permute-start(bf16[64,512]{1,0:T(8,128)(2,1)S(1)} %get-tuple-element.60.refs_0_), channel_id=1, source_target_pairs={{0,4},{1,5},{2,6},{3,7},{4,0},{5,1},{6,2},{7,3},{8,12},{9,13},{10,... | collective-permute-start | bytes 196616 | tf_op jit(solution)/shard_map/ppermute | solution.py:17
  93.3 3.5 %collective-permute-start.26 = (bf16[64,512]{1,0:T(8,128)(2,1)S(1)}, bf16[64,512]{1,0:T(8,128)(2,1)S(1)}, u32[]{:S(2)}, u32[]{:S(2)}) collective-permute-start(bf16[64,512]{1,0:T(8,128)(2,1)S(1)} %collective-permute-done.23.refs_1_), channel_id=1, source_target_pairs={{0,4},{1,5},{2,6},{3,7},{4,0},{5,1},{6,2},{7,3},{8,12},{9,13},{10,... | collective-permute-start | bytes 196616 | tf_op jit(solution)/shard_map/ppermute | solution.py:17
  98.7 2.3 %collective-permute-start.30 = (bf16[128,512]{1,0:T(8,128)(2,1)S(1)}, bf16[128,512]{1,0:T(8,128)(2,1)S(1)}, u32[]{:S(2)}, u32[]{:S(2)}) collective-permute-start(bf16[128,512]{1,0:T(8,128)(2,1)S(1)} %shard_map.71), channel_id=1, source_target_pairs={{0,3},{1,2},{2,1},{3,0},{4,7},{5,6},{6,5},{7,4},{8,11},{9,10},{10,... | collective-permute-start | bytes 393224 | tf_op jit(solution)/shard_map/ppermute | solution.py:17
  101.2 1.8 %collective-permute-done.28.refs_6_ = bf16[64,512]{1,0:T(8,128)(2,1)S(1)} collective-permute-done((bf16[64,512]{1,0:T(8,128)(2,1)S(1)}, bf16[64,512]{1,0:T(8,128)(2,1)S(1)}, u32[]{:S(2)}, u32[]{:S(2)}) %collective-permute-start.28) | collective-permute-done | bytes 65568 | tf_op jit(solution)/shard_map/ppermute | solution.py:17
  103.1 2.2 %collective-permute-done.31.refs_9_ = bf16[64,512]{1,0:T(8,128)(2,1)S(1)} collective-permute-done((bf16[64,512]{1,0:T(8,128)(2,1)S(1)}, bf16[64,512]{1,0:T(8,128)(2,1)S(1)}, u32[]{:S(2)}, u32[]{:S(2)}) %collective-permute-start.31) | collective-permute-done | bytes 65568 | tf_op jit(solution)/shard_map/ppermute | solution.py:17
  107.5 2.1 %collective-permute-done.32.refs_10_ = bf16[64,512]{1,0:T(8,128)(2,1)S(1)} collective-permute-done((bf16[64,512]{1,0:T(8,128)(2,1)S(1)}, bf16[64,512]{1,0:T(8,128)(2,1)S(1)}, u32[]{:S(2)}, u32[]{:S(2)}) %collective-permute-start.32) | collective-permute-done | bytes 65568 | tf_op jit(solution)/shard_map/ppermute | solution.py:17
  109.6 1.9 %collective-permute-done.34.refs_12_ = bf16[64,512]{1,0:T(8,128)(2,1)S(1)} collective-permute-done((bf16[64,512]{1,0:T(8,128)(2,1)S(1)}, bf16[64,512]{1,0:T(8,128)(2,1)S(1)}, u32[]{:S(2)}, u32[]{:S(2)}) %collective-permute-start.34) | collective-permute-done | bytes 65568 | tf_op jit(solution)/shard_map/ppermute | solution.py:17
  114.5 10.7 %all_to_all.5.s_ref = f32[32,1,128]{2,1,0:T(1,128)S(1)} all-to-all(f32[32,1,128]{2,1,0:T(1,128)S(1)} %get-tuple-element.66), channel_id=1, replica_groups=mesh['gen'=4,'bank'=8] {'gen','bank'}, dimensions={0} | all-to-all | bytes 32768 | tf_op jit(solution)/shard_map/all_to_all | solution.py:536
  (64 shorter events, 19.3 us)
Async XLA Ops:
  0.0 24.6 %collective-permute-start.6 = (bf16[1024,1024]{1,0:T(8,128)(2,1)}, bf16[1024,1024]{1,0:T(8,128)(2,1)S(1)}, u32[]{:S(2)}, u32[]{:S(2)}) collective-permute-start(bf16[1024,1024]{1,0:T(8,128)(2,1)} %w_hbm.1), channel_id=1, source_target_pairs={{0,8},{8,0},{16,24},{24,16},{1,9},{9,1},{17,25},{25,17},{2,10},{10... | collective-permute-start | bytes 6291464 | tf_op jit(solution)/shard_map/ppermute | solution.py:17
  3.0 11.8 %collective-permute-start.12 = (bf16[176,1024]{1,0:T(8,128)(2,1)S(1)}, bf16[176,1024]{1,0:T(8,128)(2,1)S(1)}, u32[]{:S(2)}, u32[]{:S(2)}) collective-permute-start(bf16[176,1024]{1,0:T(8,128)(2,1)S(1)} %get-tuple-element.51), channel_id=1, source_target_pairs={{0,1},{1,0},{2,3},{3,2},{4,5},{5,4},{6,7},{7,6},{8,9},{9,8},{10,11... | collective-permute-start | bytes 1081352 | tf_op jit(solution)/shard_map/ppermute | solution.py:17
  5.6 17.0 %collective-permute-start.14 = (bf16[176,1024]{1,0:T(8,128)(2,1)S(1)}, bf16[176,1024]{1,0:T(8,128)(2,1)S(1)}, u32[]{:S(2)}, u32[]{:S(2)}) collective-permute-start(bf16[176,1024]{1,0:T(8,128)(2,1)S(1)} %get-tuple-element.52), channel_id=1, source_target_pairs={{0,1},{1,0},{2,3},{3,2},{4,5},{5,4},{6,7},{7,6},{8,9},{9,8},{10,11... | collective-permute-start | bytes 1081352 | tf_op jit(solution)/shard_map/ppermute | solution.py:17
  5.7 12.8 %collective-permute-start.5 = (bf16[64,2048]{1,0:T(8,128)(2,1)S(1)}, bf16[64,2048]{1,0:T(8,128)(2,1)S(1)}, u32[]{:S(2)}, u32[]{:S(2)}) collective-permute-start(bf16[64,2048]{1,0:T(8,128)(2,1)S(1)} %get-tuple-element.43), channel_id=1, source_target_pairs={{0,16},{8,24},{16,0},{24,8},{1,17},{9,25},{17,1},{25,9},{2,18},{10... | collective-permute-start | bytes 786440 | tf_op jit(solution)/shard_map/ppermute | solution.py:17
  7.6 34.8 %collective-permute-start.17 = (bf16[320,1024]{1,0:T(8,128)(2,1)S(1)}, bf16[320,1024]{1,0:T(8,128)(2,1)S(1)}, u32[]{:S(2)}, u32[]{:S(2)}) collective-permute-start(bf16[320,1024]{1,0:T(8,128)(2,1)S(1)} %get-tuple-element.53), channel_id=1, source_target_pairs={{0,1},{1,0},{2,3},{3,2},{4,5},{5,4},{6,7},{7,6},{8,9},{9,8},{10,11... | collective-permute-start | bytes 1966088 | tf_op jit(solution)/shard_map/ppermute | solution.py:17
  14.9 10.7 %collective-permute-start.13 = (bf16[176,1024]{1,0:T(8,128)(2,1)S(1)}, bf16[176,1024]{1,0:T(8,128)(2,1)S(1)}, u32[]{:S(2)}, u32[]{:S(2)}) collective-permute-start(bf16[176,1024]{1,0:T(8,128)(2,1)S(1)} %collective-permute-done.12.refs_0_), channel_id=1, source_target_pairs={{0,16},{8,24},{16,0},{24,8},{1,17},{9,25},{17,1},{25,9},{2,18},{10... | collective-permute-start | bytes 1081352 | tf_op jit(solution)/shard_map/ppermute | solution.py:17
  18.5 7.0 %collective-permute-start = (bf16[64,1024]{1,0:T(8,128)(2,1)S(1)}, bf16[64,1024]{1,0:T(8,128)(2,1)S(1)}, u32[]{:S(2)}, u32[]{:S(2)}) collective-permute-start(bf16[64,1024]{1,0:T(8,128)(2,1)S(1)} %get-tuple-element.38), channel_id=1, source_target_pairs={{0,2},{1,3},{2,0},{3,1},{4,6},{5,7},{6,4},{7,5},{8,10},{9,11},{10,... | collective-permute-start | bytes 393224 | tf_op jit(solution)/shard_map/ppermute | solution.py:17
  22.6 19.4 %collective-permute-start.15 = (bf16[176,1024]{1,0:T(8,128)(2,1)S(1)}, bf16[176,1024]{1,0:T(8,128)(2,1)S(1)}, u32[]{:S(2)}, u32[]{:S(2)}) collective-permute-start(bf16[176,1024]{1,0:T(8,128)(2,1)S(1)} %collective-permute-done.14.refs_1_), channel_id=1, source_target_pairs={{0,16},{8,24},{16,0},{24,8},{1,17},{9,25},{17,1},{25,9},{2,18},{10... | collective-permute-start | bytes 1081352 | tf_op jit(solution)/shard_map/ppermute | solution.py:17
  24.7 43.2 %collective-permute-start.19 = (bf16[352,1024]{1,0:T(8,128)(2,1)S(1)}, bf16[352,1024]{1,0:T(8,128)(2,1)S(1)}, u32[]{:S(2)}, u32[]{:S(2)}) collective-permute-start(bf16[352,1024]{1,0:T(8,128)(2,1)S(1)} %shard_map.66.refs_2_), channel_id=1, source_target_pairs={{0,8},{8,0},{16,24},{24,16},{1,9},{9,1},{17,25},{25,17},{2,10},{10... | collective-permute-start | bytes 2162696 | tf_op jit(solution)/shard_map/ppermute | solution.py:17
  25.5 12.8 %collective-permute-start.7 = (f32[64,1024]{1,0:T(8,128)S(1)}, f32[64,1024]{1,0:T(8,128)S(1)}, u32[]{:S(2)}, u32[]{:S(2)}) collective-permute-start(f32[64,1024]{1,0:T(8,128)S(1)} %get-tuple-element.47), channel_id=1, source_target_pairs={{0,16},{8,24},{16,0},{24,8},{1,17},{9,25},{17,1},{25,9},{2,18},{10... | collective-permute-start | bytes 786440 | tf_op jit(solution)/shard_map/ppermute | solution.py:17
  25.6 16.8 %collective-permute-start.1 = (bf16[64,1024]{1,0:T(8,128)(2,1)S(1)}, bf16[64,1024]{1,0:T(8,128)(2,1)S(1)}, u32[]{:S(2)}, u32[]{:S(2)}) collective-permute-start(bf16[64,1024]{1,0:T(8,128)(2,1)S(1)} %get-tuple-element.39), channel_id=1, source_target_pairs={{0,4},{1,5},{2,6},{3,7},{4,0},{5,1},{6,2},{7,3},{8,12},{9,13},{10,... | collective-permute-start | bytes 393224 | tf_op jit(solution)/shard_map/ppermute | solution.py:17
  38.3 7.5 %collective-permute-start.2 = (bf16[64,1024]{1,0:T(8,128)(2,1)S(1)}, bf16[64,1024]{1,0:T(8,128)(2,1)S(1)}, u32[]{:S(2)}, u32[]{:S(2)}) collective-permute-start(bf16[64,1024]{1,0:T(8,128)(2,1)S(1)} %get-tuple-element.40), channel_id=1, source_target_pairs={{0,6},{1,7},{2,4},{3,5},{4,2},{5,3},{6,0},{7,1},{8,14},{9,15},{10,... | collective-permute-start | bytes 393224 | tf_op jit(solution)/shard_map/ppermute | solution.py:17
  42.0 8.6 %collective-permute-start.10 = (bf16[64,1024]{1,0:T(8,128)(2,1)S(1)}, bf16[64,1024]{1,0:T(8,128)(2,1)S(1)}, u32[]{:S(2)}, u32[]{:S(2)}) collective-permute-start(bf16[64,1024]{1,0:T(8,128)(2,1)S(1)} %get-tuple-element.48.refs_0_.unit_ref), channel_id=1, source_target_pairs={{0,6},{1,7},{2,4},{3,5},{4,2},{5,3},{6,0},{7,1},{8,14},{9,15},{10,... | collective-permute-start | bytes 393224 | tf_op jit(solution)/shard_map/ppermute | solution.py:17
  42.4 30.7 %collective-permute-start.16 = (bf16[352,1024]{1,0:T(8,128)(2,1)S(1)}, bf16[352,1024]{1,0:T(8,128)(2,1)S(1)}, u32[]{:S(2)}, u32[]{:S(2)}) collective-permute-start(bf16[352,1024]{1,0:T(8,128)(2,1)S(1)} %shard_map.64.refs_1_), channel_id=1, source_target_pairs={{0,8},{8,0},{16,24},{24,16},{1,9},{9,1},{17,25},{25,17},{2,10},{10... | collective-permute-start | bytes 2162696 | tf_op jit(solution)/shard_map/ppermute | solution.py:17
  42.5 30.6 %collective-permute-start.18 = (bf16[320,1024]{1,0:T(8,128)(2,1)S(1)}, bf16[320,1024]{1,0:T(8,128)(2,1)S(1)}, u32[]{:S(2)}, u32[]{:S(2)}) collective-permute-start(bf16[320,1024]{1,0:T(8,128)(2,1)S(1)} %collective-permute-done.17.refs_2_), channel_id=1, source_target_pairs={{0,8},{8,0},{16,24},{24,16},{1,9},{9,1},{17,25},{25,17},{2,10},{10... | collective-permute-start | bytes 1966088 | tf_op jit(solution)/shard_map/ppermute | solution.py:17
  45.7 9.0 %collective-permute-start.8 = (bf16[64,1024]{1,0:T(8,128)(2,1)S(1)}, bf16[64,1024]{1,0:T(8,128)(2,1)S(1)}, u32[]{:S(2)}, u32[]{:S(2)}) collective-permute-start(bf16[64,1024]{1,0:T(8,128)(2,1)S(1)} %get-tuple-element.48.refs_0_.unit_ref), channel_id=1, source_target_pairs={{0,2},{1,3},{2,0},{3,1},{4,6},{5,7},{6,4},{7,5},{8,10},{9,11},{10,... | collective-permute-start | bytes 393224 | tf_op jit(solution)/shard_map/ppermute | solution.py:17
  50.5 15.6 %collective-permute-start.3 = (bf16[256,512]{1,0:T(8,128)(2,1)S(1)}, bf16[256,512]{1,0:T(8,128)(2,1)S(1)}, u32[]{:S(2)}, u32[]{:S(2)}) collective-permute-start(bf16[256,512]{1,0:T(8,128)(2,1)S(1)} %get-tuple-element.42), channel_id=1, source_target_pairs={{0,1},{1,0},{2,3},{3,2},{4,5},{5,4},{6,7},{7,6},{8,9},{9,8},{10,11... | collective-permute-start | bytes 786440 | tf_op jit(solution)/shard_map/ppermute | solution.py:17
  54.7 7.3 %collective-permute-start.9 = (bf16[64,1024]{1,0:T(8,128)(2,1)S(1)}, bf16[64,1024]{1,0:T(8,128)(2,1)S(1)}, u32[]{:S(2)}, u32[]{:S(2)}) collective-permute-start(bf16[64,1024]{1,0:T(8,128)(2,1)S(1)} %get-tuple-element.48.refs_0_.unit_ref), channel_id=1, source_target_pairs={{0,4},{1,5},{2,6},{3,7},{4,0},{5,1},{6,2},{7,3},{8,12},{9,13},{10,... | collective-permute-start | bytes 393224 | tf_op jit(solution)/shard_map/ppermute | solution.py:17
  62.0 16.9 %collective-permute-start.11 = (bf16[256,1024]{1,0:T(8,128)(2,1)S(1)}, bf16[256,1024]{1,0:T(8,128)(2,1)S(1)}, u32[]{:S(2)}, u32[]{:S(2)}) collective-permute-start(bf16[256,1024]{1,0:T(8,128)(2,1)S(1)} %shard_map.61.line_ref.refs_0_), channel_id=1, source_target_pairs={{0,1},{1,0},{2,3},{3,2},{4,5},{5,4},{6,7},{7,6},{8,9},{9,8},{10,11... | collective-permute-start | bytes 1572872 | tf_op jit(solution)/shard_map/ppermute | solution.py:17
  66.3 31.2 %collective-permute-start.4 = (bf16[512,512]{1,0:T(8,128)(2,1)S(1)}, bf16[512,512]{1,0:T(8,128)(2,1)S(1)}, u32[]{:S(2)}, u32[]{:S(2)}) collective-permute-start(bf16[512,512]{1,0:T(8,128)(2,1)S(1)} %shard_map.58.own_ref), channel_id=1, source_target_pairs={{0,16},{8,24},{16,0},{24,8},{1,17},{9,25},{17,1},{25,9},{2,18},{10... | collective-permute-start | bytes 1572872 | tf_op jit(solution)/shard_map/ppermute | solution.py:17
  74.5 5.2 %collective-permute-start.20 = (bf16[64,1024]{1,0:T(8,128)(2,1)S(1)}, bf16[64,1024]{1,0:T(8,128)(2,1)S(1)}, u32[]{:S(2)}, u32[]{:S(2)}) collective-permute-start(bf16[64,1024]{1,0:T(8,128)(2,1)S(1)} %get-tuple-element.57), channel_id=1, source_target_pairs={{0,2},{1,3},{2,0},{3,1},{4,6},{5,7},{6,4},{7,5},{8,10},{9,11},{10,... | collective-permute-start | bytes 393224 | tf_op jit(solution)/shard_map/ppermute | solution.py:17
  75.0 11.5 %collective-permute-start.21 = (bf16[64,1024]{1,0:T(8,128)(2,1)S(1)}, bf16[64,1024]{1,0:T(8,128)(2,1)S(1)}, u32[]{:S(2)}, u32[]{:S(2)}) collective-permute-start(bf16[64,1024]{1,0:T(8,128)(2,1)S(1)} %get-tuple-element.58), channel_id=1, source_target_pairs={{0,4},{1,5},{2,6},{3,7},{4,0},{5,1},{6,2},{7,3},{8,12},{9,13},{10,... | collective-permute-start | bytes 393224 | tf_op jit(solution)/shard_map/ppermute | solution.py:17
  76.6 9.9 %collective-permute-start.22 = (bf16[64,1024]{1,0:T(8,128)(2,1)S(1)}, bf16[64,1024]{1,0:T(8,128)(2,1)S(1)}, u32[]{:S(2)}, u32[]{:S(2)}) collective-permute-start(bf16[64,1024]{1,0:T(8,128)(2,1)S(1)} %get-tuple-element.59), channel_id=1, source_target_pairs={{0,6},{1,7},{2,4},{3,5},{4,2},{5,3},{6,0},{7,1},{8,14},{9,15},{10,... | collective-permute-start | bytes 393224 | tf_op jit(solution)/shard_map/ppermute | solution.py:17
  86.7 6.6 %collective-permute-start.23 = (bf16[64,512]{1,0:T(8,128)(2,1)S(1)}, bf16[64,512]{1,0:T(8,128)(2,1)S(1)}, u32[]{:S(2)}, u32[]{:S(2)}) collective-permute-start(bf16[64,512]{1,0:T(8,128)(2,1)S(1)} %get-tuple-element.61), channel_id=1, source_target_pairs={{0,16},{8,24},{16,0},{24,8},{1,17},{9,25},{17,1},{25,9},{2,18},{10... | collective-permute-start | bytes 196616 | tf_op jit(solution)/shard_map/ppermute | solution.py:17
  86.8 10.8 %collective-permute-start.25 = (bf16[64,512]{1,0:T(8,128)(2,1)S(1)}, bf16[64,512]{1,0:T(8,128)(2,1)S(1)}, u32[]{:S(2)}, u32[]{:S(2)}) collective-permute-start(bf16[64,512]{1,0:T(8,128)(2,1)S(1)} %get-tuple-element.60.refs_0_), channel_id=1, source_target_pairs={{0,4},{1,5},{2,6},{3,7},{4,0},{5,1},{6,2},{7,3},{8,12},{9,13},{10,... | collective-permute-start | bytes 196616 | tf_op jit(solution)/shard_map/ppermute | solution.py:17
  92.6 6.1 %collective-permute-start.27 = (bf16[64,512]{1,0:T(8,128)(2,1)S(1)}, bf16[64,512]{1,0:T(8,128)(2,1)S(1)}, u32[]{:S(2)}, u32[]{:S(2)}) collective-permute-start(bf16[64,512]{1,0:T(8,128)(2,1)S(1)} %get-tuple-element.60.refs_0_), channel_id=1, source_target_pairs={{0,6},{1,7},{2,4},{3,5},{4,2},{5,3},{6,0},{7,1},{8,14},{9,15},{10,... | collective-permute-start | bytes 196616 | tf_op jit(solution)/shard_map/ppermute | solution.py:17
  93.3 7.7 %collective-permute-start.26 = (bf16[64,512]{1,0:T(8,128)(2,1)S(1)}, bf16[64,512]{1,0:T(8,128)(2,1)S(1)}, u32[]{:S(2)}, u32[]{:S(2)}) collective-permute-start(bf16[64,512]{1,0:T(8,128)(2,1)S(1)} %collective-permute-done.23.refs_1_), channel_id=1, source_target_pairs={{0,4},{1,5},{2,6},{3,7},{4,0},{5,1},{6,2},{7,3},{8,12},{9,13},{10,... | collective-permute-start | bytes 196616 | tf_op jit(solution)/shard_map/ppermute | solution.py:17
  96.8 6.2 %collective-permute-start.28 = (bf16[64,512]{1,0:T(8,128)(2,1)S(1)}, bf16[64,512]{1,0:T(8,128)(2,1)S(1)}, u32[]{:S(2)}, u32[]{:S(2)}) collective-permute-start(bf16[64,512]{1,0:T(8,128)(2,1)S(1)} %collective-permute-done.23.refs_1_), channel_id=1, source_target_pairs={{0,6},{1,7},{2,4},{3,5},{4,2},{5,3},{6,0},{7,1},{8,14},{9,15},{10,... | collective-permute-start | bytes 196616 | tf_op jit(solution)/shard_map/ppermute | solution.py:17
  97.5 10.0 %collective-permute-start.24 = (bf16[128,512]{1,0:T(8,128)(2,1)S(1)}, bf16[128,512]{1,0:T(8,128)(2,1)S(1)}, u32[]{:S(2)}, u32[]{:S(2)}) collective-permute-start(bf16[128,512]{1,0:T(8,128)(2,1)S(1)} %shard_map.71), channel_id=1, source_target_pairs={{0,2},{1,3},{2,0},{3,1},{4,6},{5,7},{6,4},{7,5},{8,10},{9,11},{10,... | collective-permute-start | bytes 393224 | tf_op jit(solution)/shard_map/ppermute | solution.py:17
  97.6 9.9 %collective-permute-start.29 = (bf16[128,512]{1,0:T(8,128)(2,1)S(1)}, bf16[128,512]{1,0:T(8,128)(2,1)S(1)}, u32[]{:S(2)}, u32[]{:S(2)}) collective-permute-start(bf16[128,512]{1,0:T(8,128)(2,1)S(1)} %shard_map.71), channel_id=1, source_target_pairs={{0,1},{1,0},{2,3},{3,2},{4,5},{5,4},{6,7},{7,6},{8,9},{9,8},{10,11... | collective-permute-start | bytes 393224 | tf_op jit(solution)/shard_map/ppermute | solution.py:17
  98.7 8.8 %collective-permute-start.30 = (bf16[128,512]{1,0:T(8,128)(2,1)S(1)}, bf16[128,512]{1,0:T(8,128)(2,1)S(1)}, u32[]{:S(2)}, u32[]{:S(2)}) collective-permute-start(bf16[128,512]{1,0:T(8,128)(2,1)S(1)} %shard_map.71), channel_id=1, source_target_pairs={{0,3},{1,2},{2,1},{3,0},{4,7},{5,6},{6,5},{7,4},{8,11},{9,10},{10,... | collective-permute-start | bytes 393224 | tf_op jit(solution)/shard_map/ppermute | solution.py:17
  113.7 11.6 %collective-permute-start.36 = (f32[128,512]{1,0:T(8,128)S(1)}, f32[128,512]{1,0:T(8,128)S(1)}, u32[]{:S(2)}, u32[]{:S(2)}) collective-permute-start(f32[128,512]{1,0:T(8,128)S(1)} %get-tuple-element.65), channel_id=1, source_target_pairs={{0,16},{8,24},{16,0},{24,8},{1,17},{9,25},{17,1},{25,9},{2,18},{10... | collective-permute-start | bytes 786440 | tf_op jit(solution)/shard_map/ppermute | solution.py:17
  (5 other events, 18.7 us)

commit v2 on v1

--- a/solution.py
+++ b/solution.py
@@ -223,14 +223,16 @@
 
 
 def join(pieces):
-    samples, width = pieces[0].shape
-    count = len(pieces)
+    width = pieces[0].shape[1]
+    heights = [piece.shape[0] for piece in pieces]
 
     def body(*refs):
-        for i in range(count):
-            refs[-1][i * samples : (i + 1) * samples] = refs[i][...]
-
-    return call(body, pieces, [((count * samples, width), BF16)], 0)[0]
+        start = 0
+        for ref, height in zip(refs, heights):
+            refs[-1][start : start + height] = ref[...]
+            start += height
+
+    return call(body, pieces, [((sum(heights), width), BF16)], 0)[0]
 
 
 def bank_sums(line, blocks, before=None, samples=None):
@@ -504,9 +506,9 @@
     line = [unit] + [swap(unit, BANK, m) for m in evens[1:]]
     line = join(line)
     across = swap(line, BANK, 1)
-    sums = bank_sums(line, [bank_unit] + early)[0]
-    sums = bank_sums(line, middle, sums)[0]
-    far = bank_sums(line, late, sums, samples)
+    sums = bank_sums(line, [bank_unit, join(early)])[0]
+    sums = bank_sums(line, [join(middle)], sums)[0]
+    far = bank_sums(line, [join(late)], sums, samples)
     parts = [swap(v, BANK, m) for m, v in zip(evens[1:], far[1:])]
     near = pair_sums(unit, line, across)
     keep, give = embed_gradient(

time: 126 us -> 137 us (1.087)
  waiting for transfers between devices: 45.5 us -> 56.1 us
    ppermute x37, waiting for transfers between devices: 45.5 us -> 56.1 us  [swap(): return lax.ppermute(value, axis, [(i, i ^ mask) for i in range(count)])]
    pallas_call x21 -> x24, Pallas kernels: 17.7 us -> 17.5 us  [call(): pl.pallas_call(body, in_specs=[HBM if there else VMEM for there in far_aw...]
  transfers between devices with their start and end apart: 37 -> 37, of which waited for: 14 -> 18; matrix products, arithmetic and copies ran while one was open for 0% -> 0% of each run, Pallas kernels for 13% -> 12%
where the time goes in v2:
time: 137 us; the launch traced here: 136 us
  waiting for transfers between devices  56.1 us (41%)
  starting transfers between devices  51.9 us (38%)
  Pallas kernels  17.5 us (13%)
  blocking collectives  10.6 us (8%)
    ppermute x37, waiting for transfers between devices, swap(): return lax.ppermute(value, axis, [(i, i ^ mask) for i in range(count)])  56.1 us
    ppermute x37, starting transfers between devices, swap(): return lax.ppermute(value, axis, [(i, i ^ mask) for i in range(count)])  51.9 us
    pallas_call x24, Pallas kernels, call(): pl.pallas_call(body, in_specs=[HBM if there else VMEM for there in far_aw...  17.5 us
    all_to_all x1, blocking collectives, local(): squares = lax.all_to_all(squares, (GEN, BANK), 0, 0, tiled=True)  10.6 us
  transfers between devices with their start and end apart: 37, of which 18 were waited for; matrix products, arithmetic and copies ran while one was open for 0% of the time, Pallas kernels for 12%

profile of v2, /device:TPU:0, one launch (start us, length us, event | category | flops | bytes accessed | tf_op | source)
XLA Modules:
  0.0 136.3 jit_solution(3098964282844695407)
XLA Ops:
  0.5 2.0 %shard_map.55 = (bf16[64,4096]{1,0:T(8,128)(2,1)S(1)}, bf16[64,2048]{1,0:T(8,128)(2,1)S(1)}, bf16[64,2048]{1,0:T(8,128)(2,1)S(1)}, bf16[352,1024]{1,0:T(8,128)(2,1)S(1)}, bf16[320,1024]{1,0:T(8,128)(2,1)S(1)}) custom-call(bf16[64,4096]{1,0:T(8,128)(2,1)} %refs_0_.1, bf16[64,4096]{1,0:T(8,128)(2,1)} %refs_1_.1, bf16[64,4096]{1,0:T(8,128)(2,1)} %refs_2_.1, ...), custom_call_target="tpu_custom_call" | custom-call | flops 2097152 | bytes 5767168 | tf_op jit(solution)/shard_map/pallas_call | solution.py:33
  3.0 2.6 %collective-permute-start.12 = (bf16[176,1024]{1,0:T(8,128)(2,1)S(1)}, bf16[176,1024]{1,0:T(8,128)(2,1)S(1)}, u32[]{:S(2)}, u32[]{:S(2)}) collective-permute-start(bf16[176,1024]{1,0:T(8,128)(2,1)S(1)} %get-tuple-element.51), channel_id=1, source_target_pairs={{0,1},{1,0},{2,3},{3,2},{4,5},{5,4},{6,7},{7,6},{8,9},{9,8},{10,11... | collective-permute-start | bytes 1081352 | tf_op jit(solution)/shard_map/ppermute | solution.py:17
  5.7 1.9 %collective-permute-start.17 = (bf16[320,1024]{1,0:T(8,128)(2,1)S(1)}, bf16[320,1024]{1,0:T(8,128)(2,1)S(1)}, u32[]{:S(2)}, u32[]{:S(2)}) collective-permute-start(bf16[320,1024]{1,0:T(8,128)(2,1)S(1)} %get-tuple-element.53), channel_id=1, source_target_pairs={{0,1},{1,0},{2,3},{3,2},{4,5},{5,4},{6,7},{7,6},{8,9},{9,8},{10,11... | collective-permute-start | bytes 1966088 | tf_op jit(solution)/shard_map/ppermute | solution.py:17
  7.6 7.2 %collective-permute-done.12.refs_0_ = bf16[176,1024]{1,0:T(8,128)(2,1)S(1)} collective-permute-done((bf16[176,1024]{1,0:T(8,128)(2,1)S(1)}, bf16[176,1024]{1,0:T(8,128)(2,1)S(1)}, u32[]{:S(2)}, u32[]{:S(2)}) %collective-permute-start.12) | collective-permute-done | bytes 360480 | tf_op jit(solution)/shard_map/ppermute | solution.py:17
  14.9 2.0 %collective-permute-start.13 = (bf16[176,1024]{1,0:T(8,128)(2,1)S(1)}, bf16[176,1024]{1,0:T(8,128)(2,1)S(1)}, u32[]{:S(2)}, u32[]{:S(2)}) collective-permute-start(bf16[176,1024]{1,0:T(8,128)(2,1)S(1)} %collective-permute-done.12.refs_0_), channel_id=1, source_target_pairs={{0,16},{8,24},{16,0},{24,8},{1,17},{9,25},{17,1},{25,9},{2,18},{10... | collective-permute-start | bytes 1081352 | tf_op jit(solution)/shard_map/ppermute | solution.py:17
  16.9 5.7 %collective-permute-done.14.refs_1_ = bf16[176,1024]{1,0:T(8,128)(2,1)S(1)} collective-permute-done((bf16[176,1024]{1,0:T(8,128)(2,1)S(1)}, bf16[176,1024]{1,0:T(8,128)(2,1)S(1)}, u32[]{:S(2)}, u32[]{:S(2)}) %collective-permute-start.14) | collective-permute-done | bytes 360480 | tf_op jit(solution)/shard_map/ppermute | solution.py:17
  22.6 2.0 %collective-permute-start.15 = (bf16[176,1024]{1,0:T(8,128)(2,1)S(1)}, bf16[176,1024]{1,0:T(8,128)(2,1)S(1)}, u32[]{:S(2)}, u32[]{:S(2)}) collective-permute-start(bf16[176,1024]{1,0:T(8,128)(2,1)S(1)} %collective-permute-done.14.refs_1_), channel_id=1, source_target_pairs={{0,16},{8,24},{16,0},{24,8},{1,17},{9,25},{17,1},{25,9},{2,18},{10... | collective-permute-start | bytes 1081352 | tf_op jit(solution)/shard_map/ppermute | solution.py:17
  24.9 8.9 %collective-permute-done.15.refs_1_ = bf16[176,1024]{1,0:T(8,128)(2,1)S(1)} collective-permute-done((bf16[176,1024]{1,0:T(8,128)(2,1)S(1)}, bf16[176,1024]{1,0:T(8,128)(2,1)S(1)}, u32[]{:S(2)}, u32[]{:S(2)}) %collective-permute-start.15) | collective-permute-done | bytes 360480 | tf_op jit(solution)/shard_map/ppermute | solution.py:17
  34.0 1.6 %shard_map.56 = (bf16[1024,1024]{1,0:T(8,128)(2,1)S(1)}, bf16[64,1024]{1,0:T(8,128)(2,1)S(1)}, bf16[64,1024]{1,0:T(8,128)(2,1)S(1)}, bf16[64,1024]{1,0:T(8,128)(2,1)S(1)}, bf16[64,1024]{1,0:T(8,128)(2,1)S(1)}) custom-call(bf16[64,4096]{1,0:T(8,128)(2,1)S(1)} %get-tuple-element.36.hid_ref, bf16[1024,1024]{1,0:T(8,128)(2,1)} %w_hbm.1), custom_call_target="tpu_custom_call" | custom-call | bytes 2621440 | tf_op jit(solution)/shard_map/pallas_call | solution.py:33
  35.6 2.7 %collective-permute-done.5.x_ref = bf16[64,2048]{1,0:T(8,128)(2,1)S(1)} collective-permute-done((bf16[64,2048]{1,0:T(8,128)(2,1)S(1)}, bf16[64,2048]{1,0:T(8,128)(2,1)S(1)}, u32[]{:S(2)}, u32[]{:S(2)}) %collective-permute-start.5) | collective-permute-done | bytes 262176 | tf_op jit(solution)/shard_map/ppermute | solution.py:17
  40.5 1.6 %collective-permute-start = (bf16[64,1024]{1,0:T(8,128)(2,1)S(1)}, bf16[64,1024]{1,0:T(8,128)(2,1)S(1)}, u32[]{:S(2)}, u32[]{:S(2)}) collective-permute-start(bf16[64,1024]{1,0:T(8,128)(2,1)S(1)} %get-tuple-element.38), channel_id=1, source_target_pairs={{0,2},{1,3},{2,0},{3,1},{4,6},{5,7},{6,4},{7,5},{8,10},{9,11},{10,... | collective-permute-start | bytes 393224 | tf_op jit(solution)/shard_map/ppermute | solution.py:17
  42.1 3.4 %collective-permute-done.refs_1_ = bf16[64,1024]{1,0:T(8,128)(2,1)S(1)} collective-permute-done((bf16[64,1024]{1,0:T(8,128)(2,1)S(1)}, bf16[64,1024]{1,0:T(8,128)(2,1)S(1)}, u32[]{:S(2)}, u32[]{:S(2)}) %collective-permute-start) | collective-permute-done | bytes 131104 | tf_op jit(solution)/shard_map/ppermute | solution.py:17
  45.5 2.8 %collective-permute-start.1 = (bf16[64,1024]{1,0:T(8,128)(2,1)S(1)}, bf16[64,1024]{1,0:T(8,128)(2,1)S(1)}, u32[]{:S(2)}, u32[]{:S(2)}) collective-permute-start(bf16[64,1024]{1,0:T(8,128)(2,1)S(1)} %get-tuple-element.39), channel_id=1, source_target_pairs={{0,4},{1,5},{2,6},{3,7},{4,0},{5,1},{6,2},{7,3},{8,12},{9,13},{10,... | collective-permute-start | bytes 393224 | tf_op jit(solution)/shard_map/ppermute | solution.py:17
  49.5 6.5 %collective-permute-done.1.refs_2_ = bf16[64,1024]{1,0:T(8,128)(2,1)S(1)} collective-permute-done((bf16[64,1024]{1,0:T(8,128)(2,1)S(1)}, bf16[64,1024]{1,0:T(8,128)(2,1)S(1)}, u32[]{:S(2)}, u32[]{:S(2)}) %collective-permute-start.1) | collective-permute-done | bytes 131104 | tf_op jit(solution)/shard_map/ppermute | solution.py:17
  56.0 3.1 %collective-permute-start.10 = (bf16[64,1024]{1,0:T(8,128)(2,1)S(1)}, bf16[64,1024]{1,0:T(8,128)(2,1)S(1)}, u32[]{:S(2)}, u32[]{:S(2)}) collective-permute-start(bf16[64,1024]{1,0:T(8,128)(2,1)S(1)} %get-tuple-element.48.refs_0_.unit_ref), channel_id=1, source_target_pairs={{0,6},{1,7},{2,4},{3,5},{4,2},{5,3},{6,0},{7,1},{8,14},{9,15},{10,... | collective-permute-start | bytes 393224 | tf_op jit(solution)/shard_map/ppermute | solution.py:17
  60.6 3.5 %collective-permute-done.10.refs_3_ = bf16[64,1024]{1,0:T(8,128)(2,1)S(1)} collective-permute-done((bf16[64,1024]{1,0:T(8,128)(2,1)S(1)}, bf16[64,1024]{1,0:T(8,128)(2,1)S(1)}, u32[]{:S(2)}, u32[]{:S(2)}) %collective-permute-start.10) | collective-permute-done | bytes 131104 | tf_op jit(solution)/shard_map/ppermute | solution.py:17
  64.1 1.5 %collective-permute-start.3 = (bf16[256,512]{1,0:T(8,128)(2,1)S(1)}, bf16[256,512]{1,0:T(8,128)(2,1)S(1)}, u32[]{:S(2)}, u32[]{:S(2)}) collective-permute-start(bf16[256,512]{1,0:T(8,128)(2,1)S(1)} %get-tuple-element.42), channel_id=1, source_target_pairs={{0,1},{1,0},{2,3},{3,2},{4,5},{5,4},{6,7},{7,6},{8,9},{9,8},{10,11... | collective-permute-start | bytes 786440 | tf_op jit(solution)/shard_map/ppermute | solution.py:17
  65.7 3.0 %collective-permute-start.9 = (bf16[64,1024]{1,0:T(8,128)(2,1)S(1)}, bf16[64,1024]{1,0:T(8,128)(2,1)S(1)}, u32[]{:S(2)}, u32[]{:S(2)}) collective-permute-start(bf16[64,1024]{1,0:T(8,128)(2,1)S(1)} %get-tuple-element.48.refs_0_.unit_ref), channel_id=1, source_target_pairs={{0,4},{1,5},{2,6},{3,7},{4,0},{5,1},{6,2},{7,3},{8,12},{9,13},{10,... | collective-permute-start | bytes 393224 | tf_op jit(solution)/shard_map/ppermute | solution.py:17
  68.6 3.7 %collective-permute-done.9.refs_2_ = bf16[64,1024]{1,0:T(8,128)(2,1)S(1)} collective-permute-done((bf16[64,1024]{1,0:T(8,128)(2,1)S(1)}, bf16[64,1024]{1,0:T(8,128)(2,1)S(1)}, u32[]{:S(2)}, u32[]{:S(2)}) %collective-permute-start.9) | collective-permute-done | bytes 131104 | tf_op jit(solution)/shard_map/ppermute | solution.py:17
  72.3 1.6 %collective-permute-start.11 = (bf16[256,1024]{1,0:T(8,128)(2,1)S(1)}, bf16[256,1024]{1,0:T(8,128)(2,1)S(1)}, u32[]{:S(2)}, u32[]{:S(2)}) collective-permute-start(bf16[256,1024]{1,0:T(8,128)(2,1)S(1)} %shard_map.61.line_ref.refs_0_), channel_id=1, source_target_pairs={{0,1},{1,0},{2,3},{3,2},{4,5},{5,4},{6,7},{7,6},{8,9},{9,8},{10,11... | collective-permute-start | bytes 1572872 | tf_op jit(solution)/shard_map/ppermute | solution.py:17
  73.9 2.8 %shard_map.67.refs_1_ = bf16[2048,1024]{1,0:T(8,128)(2,1)S(1)} custom-call(bf16[2048,1024]{1,0:T(8,128)(2,1)} %x_hbm.1), custom_call_target="tpu_custom_call" | custom-call | flops 16777216 | bytes 4194304 | tf_op jit(solution)/shard_map/pallas_call | solution.py:33
  77.0 2.5 %collective-permute-start.4 = (bf16[512,512]{1,0:T(8,128)(2,1)S(1)}, bf16[512,512]{1,0:T(8,128)(2,1)S(1)}, u32[]{:S(2)}, u32[]{:S(2)}) collective-permute-start(bf16[512,512]{1,0:T(8,128)(2,1)S(1)} %shard_map.58.own_ref), channel_id=1, source_target_pairs={{0,16},{8,24},{16,0},{24,8},{1,17},{9,25},{17,1},{25,9},{2,18},{10... | collective-permute-start | bytes 1572872 | tf_op jit(solution)/shard_map/ppermute | solution.py:17
  79.8 3.3 %shard_map.70.refs_2_ = f32[256,1024]{1,0:T(8,128)S(1)} custom-call(bf16[256,1024]{1,0:T(8,128)(2,1)S(1)} %shard_map.61.line_ref.refs_0_, bf16[2048,1024]{1,0:T(8,128)(2,1)S(1)} %shard_map.67.refs_1_, bf16[704,1024]{1,0:T(8,128)(2,1)S(1)} %shard_map.69.refs_2_), custom_call_target="tpu_custom_call" | custom-call | flops 2885681152 | bytes 6160384 | tf_op jit(solution)/shard_map/pallas_call | solution.py:33
  85.9 3.2 %collective-permute-start.21 = (bf16[64,1024]{1,0:T(8,128)(2,1)S(1)}, bf16[64,1024]{1,0:T(8,128)(2,1)S(1)}, u32[]{:S(2)}, u32[]{:S(2)}) collective-permute-start(bf16[64,1024]{1,0:T(8,128)(2,1)S(1)} %get-tuple-element.58), channel_id=1, source_target_pairs={{0,4},{1,5},{2,6},{3,7},{4,0},{5,1},{6,2},{7,3},{8,12},{9,13},{10,... | collective-permute-start | bytes 393224 | tf_op jit(solution)/shard_map/ppermute | solution.py:17
  92.1 1.5 %collective-permute-done.21.refs_5_ = bf16[64,1024]{1,0:T(8,128)(2,1)S(1)} collective-permute-done((bf16[64,1024]{1,0:T(8,128)(2,1)S(1)}, bf16[64,1024]{1,0:T(8,128)(2,1)S(1)}, u32[]{:S(2)}, u32[]{:S(2)}) %collective-permute-start.21) | collective-permute-done | bytes 131104 | tf_op jit(solution)/shard_map/ppermute | solution.py:17
  93.6 2.8 %collective-permute-done.22.refs_6_ = bf16[64,1024]{1,0:T(8,128)(2,1)S(1)} collective-permute-done((bf16[64,1024]{1,0:T(8,128)(2,1)S(1)}, bf16[64,1024]{1,0:T(8,128)(2,1)S(1)}, u32[]{:S(2)}, u32[]{:S(2)}) %collective-permute-start.22) | collective-permute-done | bytes 131104 | tf_op jit(solution)/shard_map/ppermute | solution.py:17
  96.9 6.6 %collective-permute-start.25 = (bf16[64,512]{1,0:T(8,128)(2,1)S(1)}, bf16[64,512]{1,0:T(8,128)(2,1)S(1)}, u32[]{:S(2)}, u32[]{:S(2)}) collective-permute-start(bf16[64,512]{1,0:T(8,128)(2,1)S(1)} %get-tuple-element.60.refs_0_), channel_id=1, source_target_pairs={{0,4},{1,5},{2,6},{3,7},{4,0},{5,1},{6,2},{7,3},{8,12},{9,13},{10,... | collective-permute-start | bytes 196616 | tf_op jit(solution)/shard_map/ppermute | solution.py:17
  104.0 2.9 %collective-permute-start.26 = (bf16[64,512]{1,0:T(8,128)(2,1)S(1)}, bf16[64,512]{1,0:T(8,128)(2,1)S(1)}, u32[]{:S(2)}, u32[]{:S(2)}) collective-permute-start(bf16[64,512]{1,0:T(8,128)(2,1)S(1)} %collective-permute-done.23.refs_1_), channel_id=1, source_target_pairs={{0,4},{1,5},{2,6},{3,7},{4,0},{5,1},{6,2},{7,3},{8,12},{9,13},{10,... | collective-permute-start | bytes 196616 | tf_op jit(solution)/shard_map/ppermute | solution.py:17
  109.7 2.0 %collective-permute-start.30 = (bf16[128,512]{1,0:T(8,128)(2,1)S(1)}, bf16[128,512]{1,0:T(8,128)(2,1)S(1)}, u32[]{:S(2)}, u32[]{:S(2)}) collective-permute-start(bf16[128,512]{1,0:T(8,128)(2,1)S(1)} %shard_map.74), channel_id=1, source_target_pairs={{0,3},{1,2},{2,1},{3,0},{4,7},{5,6},{6,5},{7,4},{8,11},{9,10},{10,... | collective-permute-start | bytes 393224 | tf_op jit(solution)/shard_map/ppermute | solution.py:17
  113.7 2.6 %collective-permute-done.31.refs_9_ = bf16[64,512]{1,0:T(8,128)(2,1)S(1)} collective-permute-done((bf16[64,512]{1,0:T(8,128)(2,1)S(1)}, bf16[64,512]{1,0:T(8,128)(2,1)S(1)}, u32[]{:S(2)}, u32[]{:S(2)}) %collective-permute-start.31) | collective-permute-done | bytes 65568 | tf_op jit(solution)/shard_map/ppermute | solution.py:17
  118.3 2.2 %collective-permute-done.32.refs_10_ = bf16[64,512]{1,0:T(8,128)(2,1)S(1)} collective-permute-done((bf16[64,512]{1,0:T(8,128)(2,1)S(1)}, bf16[64,512]{1,0:T(8,128)(2,1)S(1)}, u32[]{:S(2)}, u32[]{:S(2)}) %collective-permute-start.32) | collective-permute-done | bytes 65568 | tf_op jit(solution)/shard_map/ppermute | solution.py:17
  124.7 10.6 %all_to_all.5.s_ref = f32[32,1,128]{2,1,0:T(1,128)S(1)} all-to-all(f32[32,1,128]{2,1,0:T(1,128)S(1)} %get-tuple-element.66), channel_id=1, replica_groups=mesh['gen'=4,'bank'=8] {'gen','bank'}, dimensions={0} | all-to-all | bytes 32768 | tf_op jit(solution)/shard_map/all_to_all | solution.py:538
  (67 shorter events, 25.7 us)
Async XLA Ops:
  0.0 38.3 %collective-permute-start.6 = (bf16[1024,1024]{1,0:T(8,128)(2,1)}, bf16[1024,1024]{1,0:T(8,128)(2,1)S(1)}, u32[]{:S(2)}, u32[]{:S(2)}) collective-permute-start(bf16[1024,1024]{1,0:T(8,128)(2,1)} %w_hbm.1), channel_id=1, source_target_pairs={{0,8},{8,0},{16,24},{24,16},{1,9},{9,1},{17,25},{25,17},{2,10},{10... | collective-permute-start | bytes 6291464 | tf_op jit(solution)/shard_map/ppermute | solution.py:17
  3.0 11.8 %collective-permute-start.12 = (bf16[176,1024]{1,0:T(8,128)(2,1)S(1)}, bf16[176,1024]{1,0:T(8,128)(2,1)S(1)}, u32[]{:S(2)}, u32[]{:S(2)}) collective-permute-start(bf16[176,1024]{1,0:T(8,128)(2,1)S(1)} %get-tuple-element.51), channel_id=1, source_target_pairs={{0,1},{1,0},{2,3},{3,2},{4,5},{5,4},{6,7},{7,6},{8,9},{9,8},{10,11... | collective-permute-start | bytes 1081352 | tf_op jit(solution)/shard_map/ppermute | solution.py:17
  5.6 17.0 %collective-permute-start.14 = (bf16[176,1024]{1,0:T(8,128)(2,1)S(1)}, bf16[176,1024]{1,0:T(8,128)(2,1)S(1)}, u32[]{:S(2)}, u32[]{:S(2)}) collective-permute-start(bf16[176,1024]{1,0:T(8,128)(2,1)S(1)} %get-tuple-element.52), channel_id=1, source_target_pairs={{0,1},{1,0},{2,3},{3,2},{4,5},{5,4},{6,7},{7,6},{8,9},{9,8},{10,11... | collective-permute-start | bytes 1081352 | tf_op jit(solution)/shard_map/ppermute | solution.py:17
  5.7 36.4 %collective-permute-start.17 = (bf16[320,1024]{1,0:T(8,128)(2,1)S(1)}, bf16[320,1024]{1,0:T(8,128)(2,1)S(1)}, u32[]{:S(2)}, u32[]{:S(2)}) collective-permute-start(bf16[320,1024]{1,0:T(8,128)(2,1)S(1)} %get-tuple-element.53), channel_id=1, source_target_pairs={{0,1},{1,0},{2,3},{3,2},{4,5},{5,4},{6,7},{7,6},{8,9},{9,8},{10,11... | collective-permute-start | bytes 1966088 | tf_op jit(solution)/shard_map/ppermute | solution.py:17
  14.9 10.1 %collective-permute-start.13 = (bf16[176,1024]{1,0:T(8,128)(2,1)S(1)}, bf16[176,1024]{1,0:T(8,128)(2,1)S(1)}, u32[]{:S(2)}, u32[]{:S(2)}) collective-permute-start(bf16[176,1024]{1,0:T(8,128)(2,1)S(1)} %collective-permute-done.12.refs_0_), channel_id=1, source_target_pairs={{0,16},{8,24},{16,0},{24,8},{1,17},{9,25},{17,1},{25,9},{2,18},{10... | collective-permute-start | bytes 1081352 | tf_op jit(solution)/shard_map/ppermute | solution.py:17
  22.6 11.3 %collective-permute-start.15 = (bf16[176,1024]{1,0:T(8,128)(2,1)S(1)}, bf16[176,1024]{1,0:T(8,128)(2,1)S(1)}, u32[]{:S(2)}, u32[]{:S(2)}) collective-permute-start(bf16[176,1024]{1,0:T(8,128)(2,1)S(1)} %collective-permute-done.14.refs_1_), channel_id=1, source_target_pairs={{0,16},{8,24},{16,0},{24,8},{1,17},{9,25},{17,1},{25,9},{2,18},{10... | collective-permute-start | bytes 1081352 | tf_op jit(solution)/shard_map/ppermute | solution.py:17
  24.6 13.7 %collective-permute-start.5 = (bf16[64,2048]{1,0:T(8,128)(2,1)S(1)}, bf16[64,2048]{1,0:T(8,128)(2,1)S(1)}, u32[]{:S(2)}, u32[]{:S(2)}) collective-permute-start(bf16[64,2048]{1,0:T(8,128)(2,1)S(1)} %get-tuple-element.43), channel_id=1, source_target_pairs={{0,16},{8,24},{16,0},{24,8},{1,17},{9,25},{17,1},{25,9},{2,18},{10... | collective-permute-start | bytes 786440 | tf_op jit(solution)/shard_map/ppermute | solution.py:17
  24.9 54.6 %collective-permute-start.19 = (bf16[352,1024]{1,0:T(8,128)(2,1)S(1)}, bf16[352,1024]{1,0:T(8,128)(2,1)S(1)}, u32[]{:S(2)}, u32[]{:S(2)}) collective-permute-start(bf16[352,1024]{1,0:T(8,128)(2,1)S(1)} %shard_map.68.refs_0_), channel_id=1, source_target_pairs={{0,8},{8,0},{16,24},{24,16},{1,9},{9,1},{17,25},{25,17},{2,10},{10... | collective-permute-start | bytes 2162696 | tf_op jit(solution)/shard_map/ppermute | solution.py:17
  33.9 45.7 %collective-permute-start.16 = (bf16[352,1024]{1,0:T(8,128)(2,1)S(1)}, bf16[352,1024]{1,0:T(8,128)(2,1)S(1)}, u32[]{:S(2)}, u32[]{:S(2)}) collective-permute-start(bf16[352,1024]{1,0:T(8,128)(2,1)S(1)} %shard_map.64.refs_0_), channel_id=1, source_target_pairs={{0,8},{8,0},{16,24},{24,16},{1,9},{9,1},{17,25},{25,17},{2,10},{10... | collective-permute-start | bytes 2162696 | tf_op jit(solution)/shard_map/ppermute | solution.py:17
  39.0 9.3 %collective-permute-start.7 = (f32[64,1024]{1,0:T(8,128)S(1)}, f32[64,1024]{1,0:T(8,128)S(1)}, u32[]{:S(2)}, u32[]{:S(2)}) collective-permute-start(f32[64,1024]{1,0:T(8,128)S(1)} %get-tuple-element.47), channel_id=1, source_target_pairs={{0,16},{8,24},{16,0},{24,8},{1,17},{9,25},{17,1},{25,9},{2,18},{10... | collective-permute-start | bytes 786440 | tf_op jit(solution)/shard_map/ppermute | solution.py:17
  40.5 5.0 %collective-permute-start = (bf16[64,1024]{1,0:T(8,128)(2,1)S(1)}, bf16[64,1024]{1,0:T(8,128)(2,1)S(1)}, u32[]{:S(2)}, u32[]{:S(2)}) collective-permute-start(bf16[64,1024]{1,0:T(8,128)(2,1)S(1)} %get-tuple-element.38), channel_id=1, source_target_pairs={{0,2},{1,3},{2,0},{3,1},{4,6},{5,7},{6,4},{7,5},{8,10},{9,11},{10,... | collective-permute-start | bytes 393224 | tf_op jit(solution)/shard_map/ppermute | solution.py:17
  42.1 37.6 %collective-permute-start.18 = (bf16[320,1024]{1,0:T(8,128)(2,1)S(1)}, bf16[320,1024]{1,0:T(8,128)(2,1)S(1)}, u32[]{:S(2)}, u32[]{:S(2)}) collective-permute-start(bf16[320,1024]{1,0:T(8,128)(2,1)S(1)} %collective-permute-done.17.refs_1_), channel_id=1, source_target_pairs={{0,8},{8,0},{16,24},{24,16},{1,9},{9,1},{17,25},{25,17},{2,10},{10... | collective-permute-start | bytes 1966088 | tf_op jit(solution)/shard_map/ppermute | solution.py:17
  45.5 10.6 %collective-permute-start.1 = (bf16[64,1024]{1,0:T(8,128)(2,1)S(1)}, bf16[64,1024]{1,0:T(8,128)(2,1)S(1)}, u32[]{:S(2)}, u32[]{:S(2)}) collective-permute-start(bf16[64,1024]{1,0:T(8,128)(2,1)S(1)} %get-tuple-element.39), channel_id=1, source_target_pairs={{0,4},{1,5},{2,6},{3,7},{4,0},{5,1},{6,2},{7,3},{8,12},{9,13},{10,... | collective-permute-start | bytes 393224 | tf_op jit(solution)/shard_map/ppermute | solution.py:17
  48.3 10.9 %collective-permute-start.2 = (bf16[64,1024]{1,0:T(8,128)(2,1)S(1)}, bf16[64,1024]{1,0:T(8,128)(2,1)S(1)}, u32[]{:S(2)}, u32[]{:S(2)}) collective-permute-start(bf16[64,1024]{1,0:T(8,128)(2,1)S(1)} %get-tuple-element.40), channel_id=1, source_target_pairs={{0,6},{1,7},{2,4},{3,5},{4,2},{5,3},{6,0},{7,1},{8,14},{9,15},{10,... | collective-permute-start | bytes 393224 | tf_op jit(solution)/shard_map/ppermute | solution.py:17
  56.0 8.1 %collective-permute-start.10 = (bf16[64,1024]{1,0:T(8,128)(2,1)S(1)}, bf16[64,1024]{1,0:T(8,128)(2,1)S(1)}, u32[]{:S(2)}, u32[]{:S(2)}) collective-permute-start(bf16[64,1024]{1,0:T(8,128)(2,1)S(1)} %get-tuple-element.48.refs_0_.unit_ref), channel_id=1, source_target_pairs={{0,6},{1,7},{2,4},{3,5},{4,2},{5,3},{6,0},{7,1},{8,14},{9,15},{10,... | collective-permute-start | bytes 393224 | tf_op jit(solution)/shard_map/ppermute | solution.py:17
  59.1 6.5 %collective-permute-start.8 = (bf16[64,1024]{1,0:T(8,128)(2,1)S(1)}, bf16[64,1024]{1,0:T(8,128)(2,1)S(1)}, u32[]{:S(2)}, u32[]{:S(2)}) collective-permute-start(bf16[64,1024]{1,0:T(8,128)(2,1)S(1)} %get-tuple-element.48.refs_0_.unit_ref), channel_id=1, source_target_pairs={{0,2},{1,3},{2,0},{3,1},{4,6},{5,7},{6,4},{7,5},{8,10},{9,11},{10,... | collective-permute-start | bytes 393224 | tf_op jit(solution)/shard_map/ppermute | solution.py:17
  64.1 12.6 %collective-permute-start.3 = (bf16[256,512]{1,0:T(8,128)(2,1)S(1)}, bf16[256,512]{1,0:T(8,128)(2,1)S(1)}, u32[]{:S(2)}, u32[]{:S(2)}) collective-permute-start(bf16[256,512]{1,0:T(8,128)(2,1)S(1)} %get-tuple-element.42), channel_id=1, source_target_pairs={{0,1},{1,0},{2,3},{3,2},{4,5},{5,4},{6,7},{7,6},{8,9},{9,8},{10,11... | collective-permute-start | bytes 786440 | tf_op jit(solution)/shard_map/ppermute | solution.py:17
  65.7 6.6 %collective-permute-start.9 = (bf16[64,1024]{1,0:T(8,128)(2,1)S(1)}, bf16[64,1024]{1,0:T(8,128)(2,1)S(1)}, u32[]{:S(2)}, u32[]{:S(2)}) collective-permute-start(bf16[64,1024]{1,0:T(8,128)(2,1)S(1)} %get-tuple-element.48.refs_0_.unit_ref), channel_id=1, source_target_pairs={{0,4},{1,5},{2,6},{3,7},{4,0},{5,1},{6,2},{7,3},{8,12},{9,13},{10,... | collective-permute-start | bytes 393224 | tf_op jit(solution)/shard_map/ppermute | solution.py:17
  72.3 17.9 %collective-permute-start.11 = (bf16[256,1024]{1,0:T(8,128)(2,1)S(1)}, bf16[256,1024]{1,0:T(8,128)(2,1)S(1)}, u32[]{:S(2)}, u32[]{:S(2)}) collective-permute-start(bf16[256,1024]{1,0:T(8,128)(2,1)S(1)} %shard_map.61.line_ref.refs_0_), channel_id=1, source_target_pairs={{0,1},{1,0},{2,3},{3,2},{4,5},{5,4},{6,7},{7,6},{8,9},{9,8},{10,11... | collective-permute-start | bytes 1572872 | tf_op jit(solution)/shard_map/ppermute | solution.py:17
  77.0 31.1 %collective-permute-start.4 = (bf16[512,512]{1,0:T(8,128)(2,1)S(1)}, bf16[512,512]{1,0:T(8,128)(2,1)S(1)}, u32[]{:S(2)}, u32[]{:S(2)}) collective-permute-start(bf16[512,512]{1,0:T(8,128)(2,1)S(1)} %shard_map.58.own_ref), channel_id=1, source_target_pairs={{0,16},{8,24},{16,0},{24,8},{1,17},{9,25},{17,1},{25,9},{2,18},{10... | collective-permute-start | bytes 1572872 | tf_op jit(solution)/shard_map/ppermute | solution.py:17
  85.8 6.3 %collective-permute-start.20 = (bf16[64,1024]{1,0:T(8,128)(2,1)S(1)}, bf16[64,1024]{1,0:T(8,128)(2,1)S(1)}, u32[]{:S(2)}, u32[]{:S(2)}) collective-permute-start(bf16[64,1024]{1,0:T(8,128)(2,1)S(1)} %get-tuple-element.57), channel_id=1, source_target_pairs={{0,2},{1,3},{2,0},{3,1},{4,6},{5,7},{6,4},{7,5},{8,10},{9,11},{10,... | collective-permute-start | bytes 393224 | tf_op jit(solution)/shard_map/ppermute | solution.py:17
  85.9 7.7 %collective-permute-start.21 = (bf16[64,1024]{1,0:T(8,128)(2,1)S(1)}, bf16[64,1024]{1,0:T(8,128)(2,1)S(1)}, u32[]{:S(2)}, u32[]{:S(2)}) collective-permute-start(bf16[64,1024]{1,0:T(8,128)(2,1)S(1)} %get-tuple-element.58), channel_id=1, source_target_pairs={{0,4},{1,5},{2,6},{3,7},{4,0},{5,1},{6,2},{7,3},{8,12},{9,13},{10,... | collective-permute-start | bytes 393224 | tf_op jit(solution)/shard_map/ppermute | solution.py:17
  89.1 7.3 %collective-permute-start.22 = (bf16[64,1024]{1,0:T(8,128)(2,1)S(1)}, bf16[64,1024]{1,0:T(8,128)(2,1)S(1)}, u32[]{:S(2)}, u32[]{:S(2)}) collective-permute-start(bf16[64,1024]{1,0:T(8,128)(2,1)S(1)} %get-tuple-element.59), channel_id=1, source_target_pairs={{0,6},{1,7},{2,4},{3,5},{4,2},{5,3},{6,0},{7,1},{8,14},{9,15},{10,... | collective-permute-start | bytes 393224 | tf_op jit(solution)/shard_map/ppermute | solution.py:17
  96.6 7.4 %collective-permute-start.23 = (bf16[64,512]{1,0:T(8,128)(2,1)S(1)}, bf16[64,512]{1,0:T(8,128)(2,1)S(1)}, u32[]{:S(2)}, u32[]{:S(2)}) collective-permute-start(bf16[64,512]{1,0:T(8,128)(2,1)S(1)} %get-tuple-element.61), channel_id=1, source_target_pairs={{0,16},{8,24},{16,0},{24,8},{1,17},{9,25},{17,1},{25,9},{2,18},{10... | collective-permute-start | bytes 196616 | tf_op jit(solution)/shard_map/ppermute | solution.py:17
  96.9 11.3 %collective-permute-start.25 = (bf16[64,512]{1,0:T(8,128)(2,1)S(1)}, bf16[64,512]{1,0:T(8,128)(2,1)S(1)}, u32[]{:S(2)}, u32[]{:S(2)}) collective-permute-start(bf16[64,512]{1,0:T(8,128)(2,1)S(1)} %get-tuple-element.60.refs_0_), channel_id=1, source_target_pairs={{0,4},{1,5},{2,6},{3,7},{4,0},{5,1},{6,2},{7,3},{8,12},{9,13},{10,... | collective-permute-start | bytes 196616 | tf_op jit(solution)/shard_map/ppermute | solution.py:17
  103.5 6.2 %collective-permute-start.27 = (bf16[64,512]{1,0:T(8,128)(2,1)S(1)}, bf16[64,512]{1,0:T(8,128)(2,1)S(1)}, u32[]{:S(2)}, u32[]{:S(2)}) collective-permute-start(bf16[64,512]{1,0:T(8,128)(2,1)S(1)} %get-tuple-element.60.refs_0_), channel_id=1, source_target_pairs={{0,6},{1,7},{2,4},{3,5},{4,2},{5,3},{6,0},{7,1},{8,14},{9,15},{10,... | collective-permute-start | bytes 196616 | tf_op jit(solution)/shard_map/ppermute | solution.py:17
  104.0 7.7 %collective-permute-start.26 = (bf16[64,512]{1,0:T(8,128)(2,1)S(1)}, bf16[64,512]{1,0:T(8,128)(2,1)S(1)}, u32[]{:S(2)}, u32[]{:S(2)}) collective-permute-start(bf16[64,512]{1,0:T(8,128)(2,1)S(1)} %collective-permute-done.23.refs_1_), channel_id=1, source_target_pairs={{0,4},{1,5},{2,6},{3,7},{4,0},{5,1},{6,2},{7,3},{8,12},{9,13},{10,... | collective-permute-start | bytes 196616 | tf_op jit(solution)/shard_map/ppermute | solution.py:17
  106.9 6.2 %collective-permute-start.28 = (bf16[64,512]{1,0:T(8,128)(2,1)S(1)}, bf16[64,512]{1,0:T(8,128)(2,1)S(1)}, u32[]{:S(2)}, u32[]{:S(2)}) collective-permute-start(bf16[64,512]{1,0:T(8,128)(2,1)S(1)} %collective-permute-done.23.refs_1_), channel_id=1, source_target_pairs={{0,6},{1,7},{2,4},{3,5},{4,2},{5,3},{6,0},{7,1},{8,14},{9,15},{10,... | collective-permute-start | bytes 196616 | tf_op jit(solution)/shard_map/ppermute | solution.py:17
  108.1 10.2 %collective-permute-start.24 = (bf16[128,512]{1,0:T(8,128)(2,1)S(1)}, bf16[128,512]{1,0:T(8,128)(2,1)S(1)}, u32[]{:S(2)}, u32[]{:S(2)}) collective-permute-start(bf16[128,512]{1,0:T(8,128)(2,1)S(1)} %shard_map.74), channel_id=1, source_target_pairs={{0,2},{1,3},{2,0},{3,1},{4,6},{5,7},{6,4},{7,5},{8,10},{9,11},{10,... | collective-permute-start | bytes 393224 | tf_op jit(solution)/shard_map/ppermute | solution.py:17
  108.2 10.1 %collective-permute-start.29 = (bf16[128,512]{1,0:T(8,128)(2,1)S(1)}, bf16[128,512]{1,0:T(8,128)(2,1)S(1)}, u32[]{:S(2)}, u32[]{:S(2)}) collective-permute-start(bf16[128,512]{1,0:T(8,128)(2,1)S(1)} %shard_map.74), channel_id=1, source_target_pairs={{0,1},{1,0},{2,3},{3,2},{4,5},{5,4},{6,7},{7,6},{8,9},{9,8},{10,11... | collective-permute-start | bytes 393224 | tf_op jit(solution)/shard_map/ppermute | solution.py:17
  109.7 8.6 %collective-permute-start.30 = (bf16[128,512]{1,0:T(8,128)(2,1)S(1)}, bf16[128,512]{1,0:T(8,128)(2,1)S(1)}, u32[]{:S(2)}, u32[]{:S(2)}) collective-permute-start(bf16[128,512]{1,0:T(8,128)(2,1)S(1)} %shard_map.74), channel_id=1, source_target_pairs={{0,3},{1,2},{2,1},{3,0},{4,7},{5,6},{6,5},{7,4},{8,11},{9,10},{10,... | collective-permute-start | bytes 393224 | tf_op jit(solution)/shard_map/ppermute | solution.py:17
  123.9 11.5 %collective-permute-start.36 = (f32[128,512]{1,0:T(8,128)S(1)}, f32[128,512]{1,0:T(8,128)S(1)}, u32[]{:S(2)}, u32[]{:S(2)}) collective-permute-start(f32[128,512]{1,0:T(8,128)S(1)} %get-tuple-element.65), channel_id=1, source_target_pairs={{0,16},{8,24},{16,0},{24,8},{1,17},{9,25},{17,1},{25,9},{2,18},{10... | collective-permute-start | bytes 786440 | tf_op jit(solution)/shard_map/ppermute | solution.py:17
  (5 other events, 19.1 us)
